TPU v7x, 256 devices: a whole 4x4x8 slice. The times are simulated.
256 devices in a mesh: lon: 64 (over z, x_lo, y), lat: 4 (over x_hi, core).
Axes of the slice: x: 4 (x_hi: 2, x_lo: 2; x = x_hi * 2 + x_lo), y: 4, z: 8, core: 2. Of those that a mesh axis runs over, the one named last changes fastest.
Arguments:
- sketch_bits: int32 [3072, 768, 128], P('lon', 'lat'), may hold values from 0 to 1
- rates: float32 [3072, 8, 768], P('lon', None, 'lat'), may hold values from 0 to 1, as said below
- merid_matrix: bfloat16 [768, 768], P('lat'), as said below
- vert_matrix: bfloat16 [8, 8], replicated, may hold values from -2 to 2
Outputs:
- correlated: bfloat16 [3072, 768, 128], P('lon', 'lat')
Inputs may be any that keep to these rules, and one draw needn't show every extreme that they name: `rates`: rates are strictly positive. merid_matrix[j, k] is zero where |j - k| > 96.
All inputs are finite; a program needn't handle non-finite values.
Results may differ from a plain program's by a relative error of at most 0.0057.
Values may be sent and summed in bfloat16 or wider, within the bound.
A program may use at most 128 MiB of HBM per device.

v0:
```python
import jax
import jax.numpy as jnp
from jax import lax
from jax.sharding import PartitionSpec as P

BAND = 96


def with_halo(cells, sides, width):
    for axis, dim in sides:
        count = lax.axis_size(axis)
        ends = count - 1
        head = lax.slice_in_dim(cells, 0, width, axis=dim)
        tail = lax.slice_in_dim(cells, cells.shape[dim] - width, cells.shape[dim], axis=dim)
        cells = jnp.concatenate(
            [
                lax.ppermute(tail, axis, [(i, (i + 1) % count) for i in range(ends)]),
                cells,
                lax.ppermute(head, axis, [((i + 1) % count, i) for i in range(ends)]),
            ],
            axis=dim,
        )
    return cells


def expand(per_level, chan_count):
    return jnp.repeat(per_level, chan_count // per_level.shape[-1], axis=-1)


def within_slab(rate_lev, source, backward):
    rows_here = rate_lev.shape[0]
    row_ids = lax.broadcasted_iota(jnp.int32, (rows_here, rows_here), 0)
    col_ids = lax.broadcasted_iota(jnp.int32, (rows_here, rows_here), 1)
    if backward:
        lower_mask = (row_ids <= col_ids).astype(jnp.float32)
    else:
        lower_mask = (row_ids >= col_ids).astype(jnp.float32)
    cum_rate = jnp.dot(
        lower_mask,
        rate_lev.reshape(rows_here, -1),
        precision=lax.Precision.HIGHEST,
        preferred_element_type=jnp.float32,
    ).reshape(rate_lev.shape)
    cum_chan = expand(cum_rate, source.shape[-1])
    summed = jnp.dot(
        lower_mask,
        (source * jnp.exp(cum_chan)).reshape(rows_here, -1),
        precision=lax.Precision.HIGHEST,
        preferred_element_type=jnp.float32,
    ).reshape(source.shape)
    decays = jnp.exp(-cum_chan)
    inside = decays * summed
    edge_row = 0 if backward else rows_here - 1
    return (inside, decays, (cum_rate[edge_row], inside[edge_row]))


def loop_entry(rate_parts, state_parts, position, chan_count):
    device_count = rate_parts.shape[0]
    part_ids = lax.broadcasted_iota(jnp.int32, rate_parts.shape, 0)
    cum_parts = jnp.cumsum(rate_parts, axis=0)
    loop_total = cum_parts[device_count - 1]
    before_here = jnp.sum(jnp.where(part_ids < position, rate_parts, 0.0), axis=0)
    wrapped = jnp.where(part_ids >= position, 1.0, 0.0)
    exponent = before_here[None] - cum_parts + wrapped * loop_total[None]
    weights = jnp.exp(-expand(exponent, chan_count))
    collected = jnp.sum(state_parts * weights, axis=0)
    return collected / -jnp.expm1(-expand(loop_total, chan_count))


def periodic_state(own_pair, backward):
    chan_count = own_pair[1].shape[-1]
    position = lax.axis_index("lon")
    device_count = lax.axis_size("lon")
    if backward:
        rate_parts, state_parts = (
            lax.all_gather(own_pair[0][None], "lon", axis=0, tiled=True),
            lax.all_gather(own_pair[1][None], "lon", axis=0, tiled=True),
        )
        rate_parts = jnp.flip(rate_parts, axis=0)
        state_parts = jnp.flip(state_parts, axis=0)
        position = device_count - 1 - position
    else:
        rate_parts, state_parts = (
            lax.all_gather(own_pair[0][None], "lon", axis=0, tiled=True),
            lax.all_gather(own_pair[1][None], "lon", axis=0, tiled=True),
        )
    return loop_entry(rate_parts, state_parts, position, chan_count)


def per_device(sketch_bits, rates, merid_matrix, vert_matrix):
    signs = (2 * sketch_bits - 1).astype(jnp.float32)
    chan_count = signs.shape[-1]
    rate_lev = jnp.transpose(rates, (0, 2, 1))
    rate_chan = expand(rate_lev, chan_count)
    decay_chan = jnp.exp(-rate_chan)
    squared = -jnp.expm1(-2.0 * rate_chan)
    gain_in = jnp.sqrt(squared)
    gain_out = squared / jnp.sqrt(1.0 + decay_chan * decay_chan)
    inside, decays, own_pair = within_slab(rate_lev, gain_in * signs, False)
    east_state = periodic_state(own_pair, False)
    east_field = inside + decays * east_state[None]
    inside_back, decays_back, back_pair = within_slab(rate_lev, gain_out * east_field, True)
    west_state = periodic_state(back_pair, True)
    zonal_out = (inside_back + decays_back * west_state[None]).astype(jnp.bfloat16)
    lat_here = zonal_out.shape[1]
    padded = with_halo(zonal_out, (("lat", 1),), BAND)
    first_row = lax.axis_index("lat") * lat_here
    padded_rows = jnp.pad(merid_matrix, ((0, 0), (BAND, BAND)))
    band_tile = lax.dynamic_slice_in_dim(padded_rows, first_row, lat_here + 2 * BAND, 1)
    merid_out = jnp.einsum("jk,ikc->ijc", band_tile, padded, preferred_element_type=jnp.float32)
    merid_field = merid_out.astype(jnp.bfloat16)
    levels = vert_matrix.shape[0]
    columns_each = chan_count // levels
    ident_cols = jnp.eye(columns_each, dtype=jnp.bfloat16)
    level_map = (vert_matrix.T[:, None, :, None] * ident_cols[None, :, None, :]).reshape(
        chan_count, chan_count
    )
    correlated = jnp.dot(
        merid_field.reshape(-1, chan_count), level_map, preferred_element_type=jnp.float32
    )
    return correlated.reshape(merid_field.shape).astype(jnp.bfloat16)


def solution(mesh):
    in_specs = (P("lon", "lat", None), P("lon", None, "lat"), P("lat", None), P())
    out_specs = P("lon", "lat", None)
    return jax.shard_map(
        per_device, mesh=mesh, in_specs=in_specs, out_specs=out_specs, check_vma=False
    )
```

profile of v0, /device:TPU:1, one launch (start us, length us, event | category | flops | bytes accessed | tf_op | source)
XLA Modules:
  0.0 746.3 jit_solution(14948678577941122284)
XLA Ops:
  6.5 1.3 fusion.31
  7.8 1.3 copy.107
  9.2 0.6 fusion.45
  9.8 0.3 copy.113
  10.0 0.4 copy.114
  10.5 6.2 copy.112
  16.7 7.1 bitcast_multiply_fusion.1
  23.8 6.2 copy.115
  30.3 0.4 copy.111
  30.7 3.2 broadcast_in_dim.51
  33.9 6.3 copy.117
  40.2 9.2 %fusion.16 = f32[48,192,128]{2,0,1:T(8,128)S(1)} fusion(f32[48,192,128]{2,0,1:T(8,128)} %copy.117, f32[6,8,192,128]{3,2,1,0:T(8,128)} %bitcast.103), kind=kOutput, calls=%fused_computation.21 | convolution fusion | flops 680659200 | bytes 14155776 | tf_op jit(solution)/shard_map/dot_general | solution.py:45
  49.5 2.2 copy-done
  51.7 0.7 slice.40
  52.7 138.1 %all_gather.13 = f32[64,192,8]{1,2,0:T(8,128)S(1)} all-gather(f32[1,192,8]{1,2,0:T(8,128)S(1)} %copy.119), channel_id=1, replica_groups=mesh['lon'=64,'lat'=4] {'lon'}, dimensions={0}, use_global_device_ids=true | all-gather | bytes 399360 | tf_op jit(solution)/shard_map/all_gather | solution.py:84
  191.0 13.1 %fusion.47 = f32[64,192,8]{1,2,0:T(8,128)S(1)} fusion(f32[64,192,8]{1,2,0:T(8,128)S(1)} %all_gather.13), kind=kOutput, calls=%fused_computation.61 | output fusion | flops 6193152 | bytes 786432 | tf_op jit(solution)/shard_map/jit(cumsum)/reduce_window_sum | solution.py:60
  204.2 3.9 broadcast_in_dim.56
  208.1 8.8 %copy.122 = f32[64,192,128]{2,1,0:T(8,128)} copy(f32[64,192,128]{1,2,0:T(8,128)} %bitcast.98) | data formatting | bytes 12582912 | tf_op jit(solution)/shard_map/exp | solution.py:65
  217.1 0.6 fusion.46
  217.9 0.4 copy.109
  218.3 3.2 broadcast_in_dim.48
  221.5 6.4 copy.132
  228.2 0.4 copy.128
  228.6 3.2 broadcast_in_dim.58
  231.8 6.3 copy.129
  238.1 3.1 broadcast.58
  241.3 6.3 copy.126
  247.6 71.5 %all-gather.3.cloned.1.call-done = f32[64,192,128]{2,1,0:T(8,128)} async-done(((f32[1,192,128]{2,1,0:T(8,128)}), f32[64,192,128]{2,1,0:T(8,128)}) %all-gather.3.cloned.1.call-update) | async-done | bytes 6291472 | tf_op jit(solution)/shard_map/all_gather | solution.py:85
  319.2 5.4 multiply_reduce_fusion
  324.6 0.5 copy-done.2
  325.1 10.4 %fusion.19 = f32[48,192,128]{2,0,1:T(8,128)S(1)} fusion(f32[48,192,128]{2,0,1:T(8,128)} %copy.132, f32[48,192,128]{2,0,1:T(8,128)} %copy.129, f32[48,192,128]{2,0,1:T(8,128)S(1)} %copy-done.2, f32[48,192,128]{2,0,1:T(8,128)} %copy-done, f32[48,192,128]{2,0,1:T(8,128)} %copy.117, f32[192,128]{1,0:T(8,128)S(1)} %div.18), kind=kOutput, calls=%fused_computation.22 | convolution fusion | flops 685377792 | bytes 28409856 | tf_op jit(solution)/shard_map/dot_general | solution.py:45
  335.5 2.1 copy-done.1
  337.6 0.7 slice.43
  338.5 133.9 %all_gather.15 = f32[64,192,8]{1,2,0:T(8,128)S(1)} all-gather(f32[1,192,8]{1,2,0:T(8,128)S(1)} %copy.135), channel_id=1, replica_groups=mesh['lon'=64,'lat'=4] {'lon'}, dimensions={0}, use_global_device_ids=true | all-gather | bytes 399360 | tf_op jit(solution)/shard_map/all_gather | solution.py:76
  472.4 13.1 %fusion.48 = f32[64,192,8]{1,2,0:T(8,128)S(1)} fusion(f32[64,192,8]{1,2,0:T(8,128)S(1)} %rev.9), kind=kOutput, calls=%fused_computation.62 | output fusion | flops 6193152 | bytes 786432 | tf_op jit(solution)/shard_map/jit(cumsum)/reduce_window_sum | solution.py:60
  486.0 156.3 %all-gather.5.cloned.1.call-done = f32[64,192,128]{2,1,0:T(8,128)} async-done(((f32[1,192,128]{2,1,0:T(8,128)}), f32[64,192,128]{2,1,0:T(8,128)}) %all-gather.5.cloned.1.call-update) | async-done | bytes 6291472 | tf_op jit(solution)/shard_map/all_gather | solution.py:77
  642.3 8.4 %copy.134 = f32[64,192,128]{1,2,0:T(8,128)} copy(f32[64,192,128]{2,1,0:T(8,128)} %all-gather.5.cloned.1.call-done) | data formatting | bytes 12582912 | tf_op jit(solution)/shard_map/all_gather | solution.py:77
  650.8 4.3 fusion
  655.2 4.5 add_convert_fusion
  659.7 1.8 fusion.44
  661.5 49.2 %collective-permute-start = (bf16[48,96,128]{2,0,1:T(8,128)(2,1)}, bf16[48,96,128]{2,0,1:T(8,128)(2,1)S(1)}, u32[]{:S(2)}, u32[]{:S(2)}) collective-permute-start(bf16[48,96,128]{2,0,1:T(8,128)(2,1)} %get-tuple-element.5), channel_id=1, source_target_pairs={{0,1},{1,2},{2,3},{4,5},{5,6},{6,7},{8,9},{9,10},{10,11},{12,13},{... | collective-permute-start | bytes 3538952 | tf_op jit(solution)/shard_map/ppermute | solution.py:17
  710.7 1.9 collective-permute-start.1
  712.7 0.8 broadcast_multiply_fusion
  713.5 1.8 reshape.107
  715.3 8.8 %collective-permute-done = bf16[48,96,128]{2,0,1:T(8,128)(2,1)S(1)} collective-permute-done((bf16[48,96,128]{2,0,1:T(8,128)(2,1)}, bf16[48,96,128]{2,0,1:T(8,128)(2,1)S(1)}, u32[]{:S(2)}, u32[]{:S(2)}) %collective-permute-start) | collective-permute-done | bytes 1179680 | tf_op jit(solution)/shard_map/ppermute | solution.py:17
  724.1 5.9 collective-permute-done.1
  730.0 3.6 pad_maximum_fusion
  733.6 5.9 fusion.22
  (40 shorter events, 2.3 us)
Async XLA Ops:
  6.5 312.6 %all-gather.3.cloned.1.call-start = ((), (), s32[]{:S(2)}) async-start(), calls=%async_computation | async-start | bytes 6389760 | tf_op jit(solution)/shard_map/all_gather | solution.py:85
  49.4 2.2 copy-start
  52.4 589.9 %all-gather.5.cloned.1.call-start = ((), (), s32[]{:S(2)}) async-start(), calls=%async_computation.1 | async-start | bytes 6389760 | tf_op jit(solution)/shard_map/all_gather | solution.py:77
  319.2 5.9 copy-start.2
  335.5 2.1 copy-start.1
  659.7 53.0 %copy-start.3 = (bf16[8,8]{1,0:T(8,128)(2,1)S(1)}, bf16[8,8]{1,0:T(8,128)(2,1)}, u32[]{:S(2)}) copy-start(bf16[8,8]{1,0:T(8,128)(2,1)} %param.7) | copy-start | bytes 388
  661.5 62.6 %collective-permute-start = (bf16[48,96,128]{2,0,1:T(8,128)(2,1)}, bf16[48,96,128]{2,0,1:T(8,128)(2,1)S(1)}, u32[]{:S(2)}, u32[]{:S(2)}) collective-permute-start(bf16[48,96,128]{2,0,1:T(8,128)(2,1)} %get-tuple-element.5), channel_id=1, source_target_pairs={{0,1},{1,2},{2,3},{4,5},{5,6},{6,7},{8,9},{9,10},{10,11},{12,13},{... | collective-permute-start | bytes 3538952 | tf_op jit(solution)/shard_map/ppermute | solution.py:17
  710.7 19.3 %collective-permute-start.1 = (bf16[48,96,128]{2,0,1:T(8,128)(2,1)}, bf16[48,96,128]{2,0,1:T(8,128)(2,1)}, u32[]{:S(2)}, u32[]{:S(2)}) collective-permute-start(bf16[48,96,128]{2,0,1:T(8,128)(2,1)} %get-tuple-element.6), channel_id=1, source_target_pairs={{1,0},{2,1},{3,2},{5,4},{6,5},{7,6},{9,8},{10,9},{11,10},{13,12},{... | collective-permute-start | bytes 3538952 | tf_op jit(solution)/shard_map/ppermute | solution.py:19
Sparse Core Ops, SparseCore 0:
  52.5 266.5 all-gather.2
  338.5 303.7 all-gather.4
where the time goes:
time: 747 us; the launch traced here: 746 us
  blocking collectives  272 us (36%)
  waiting for transfers between devices  243 us (33%)
  local copies, waits for them, and re-layouts  86.3 us (12%)
  other arithmetic  53.8 us (7%)
  starting transfers between devices  51.1 us (7%)
  matrix products  26.7 us (4%)
  between operations  13.8 us (2%)
    all_gather x2, blocking collectives, periodic_state(): lax.all_gather(own_pair[0][None], 'lon', axis=0, tiled=True)  272 us
    all_gather x2, waiting for transfers between devices, periodic_state(): lax.all_gather(own_pair[1][None], 'lon', axis=0, tiled=True)  228 us
    ppermute x1, starting transfers between devices, with_halo(): lax.ppermute(tail, axis, [(i, (i + 1) % count) for i in range(ends)])  49.2 us
    another operation x2, other arithmetic, loop_entry(): cum_parts = jnp.cumsum(rate_parts, axis=0)  26.2 us
    dot_general x2, matrix products, within_slab(): jnp.dot(lower_mask, (source * jnp.exp(cum_chan)).reshape(rows_here, -1),...  19.6 us
    broadcast_in_dim x7, local copies, waits for them, and re-layouts, expand(): return jnp.repeat(per_level, chan_count // per_level.shape[-1], axis=-1)  16.6 us
  transfers between devices with their start and end apart: 4, of which 4 were waited for; matrix products, arithmetic and copies ran while one was open for 10% of the time, Pallas kernels for 0%

commit v1 on v0

v1 whole, which is shorter than its diff:
```python
import functools

import jax
import jax.numpy as jnp
from jax import lax
from jax.experimental import pallas as pl
from jax.experimental.pallas import tpu as pltpu
from jax.sharding import PartitionSpec as P

BAND = 96
LANES = 128
F32 = jnp.float32
BF16 = jnp.bfloat16
MESH = pl.DeviceIdType.MESH


def loss_of(rate):
    total = jnp.ones_like(rate)
    for order in range(13, 1, -1):
        total = 1.0 - total * rate * (1.0 / order)
    return rate * total


def spread(tile, index):
    return jnp.take_along_axis(tile, index, axis=1, mode="promise_in_bounds")


def lane_index(rows, first, columns_each):
    lane = lax.broadcasted_iota(jnp.int32, (rows, LANES), 1)
    return lane // columns_each + first


def filter_kernel(
    chunk,
    rates_ref,
    bits_hbm,
    ends_ref,
    inside_ref,
    coef_ref,
    coef_small_ref,
    bits,
    east,
    lev_scratch,
    lat_scratch,
    sems,
):
    lon_here, levels, lat_here = rates_ref.shape
    columns_each = LANES // levels
    per_tile = LANES // levels
    steps = lon_here // chunk
    copies = [
        pltpu.make_async_copy(
            bits_hbm.at[pl.ds(t * chunk, chunk)], bits.at[pl.ds(t * chunk, chunk)], sems.at[t]
        )
        for t in range(steps)
    ]
    for copy in copies:
        copy.start()

    loss = loss_of(rates_ref[...])
    squared = loss * (2.0 - loss)
    decay = 1.0 - loss
    lev_scratch[0] = loss
    lev_scratch[1] = squared / jnp.sqrt(1.0 + decay * decay)
    lat_scratch[0] = loss.reshape(lon_here * levels, lat_here).T
    lat_scratch[1] = jnp.sqrt(squared).reshape(lon_here * levels, lat_here).T
    lat_scratch[2] = lev_scratch[1].reshape(lon_here * levels, lat_here).T

    passed = jnp.ones((levels, lat_here), F32)
    for i in range(lon_here):
        passed = passed - lev_scratch[0, i] * passed
        lev_scratch[2, i] = passed
    coef = jnp.zeros((levels, lat_here), F32)
    lost = jnp.zeros((levels, lat_here), F32)
    for i in reversed(range(lon_here)):
        here = lev_scratch[0, i]
        coef = coef - here * coef + lev_scratch[1, i] * lev_scratch[2, i]
        lost = lost + (here - here * lost)
        lev_scratch[2, i] = coef
        lev_scratch[3, i] = lost
    coef_ref[0] = lev_scratch[2].reshape(lon_here * levels, lat_here).T
    coef_ref[1] = lev_scratch[3].reshape(lon_here * levels, lat_here).T
    coef_small_ref[...] = coef_ref[...].astype(BF16)

    def expanded(which, i):
        column = pl.multiple_of(i // per_tile * LANES, LANES)
        index = lane_index(lat_here, i % per_tile * levels, columns_each)
        return spread(lat_scratch[which, :, pl.ds(column, LANES)], index)

    def forward(i, state):
        gain = expanded(1, i)
        state = state - expanded(0, i) * state + jnp.where(bits[i] > 0, gain, -gain)
        east[i] = state
        return state

    def backward(k, state):
        i = lon_here - 1 - k
        state = state - expanded(0, i) * state + expanded(2, i) * east[i]
        inside_ref[i] = state.astype(BF16)
        return state

    state = jnp.zeros((lat_here, LANES), F32)
    for t in range(steps):
        copies[t].wait()
        state = lax.fori_loop(t * chunk, (t + 1) * chunk, forward, state)
    ends_ref[0] = state
    ends_ref[1] = lax.fori_loop(0, lon_here, backward, jnp.zeros_like(state))
    index = lane_index(lat_here, 0, columns_each)
    lane = lax.broadcasted_iota(jnp.int32, (lat_here, LANES), 1)
    first_half = lane % columns_each < columns_each // 2
    ends_ref[2] = jnp.where(
        first_half,
        spread(coef_ref[1, :, :LANES], index),
        spread(coef_ref[0, :, :LANES], index),
    )


def run_filters(rates, bits):
    lon_here, levels, lat_here = rates.shape
    chunk = 8
    vmem = pl.BlockSpec(memory_space=pltpu.VMEM)
    hbm = pl.BlockSpec(memory_space=pltpu.HBM)
    return pl.pallas_call(
        functools.partial(filter_kernel, chunk),
        name="zonal_filters",
        out_shape=(
            jax.ShapeDtypeStruct((3, lat_here, LANES), F32),
            jax.ShapeDtypeStruct((lon_here, lat_here, LANES), BF16),
            jax.ShapeDtypeStruct((2, lat_here, lon_here * levels), F32),
            jax.ShapeDtypeStruct((2, lat_here, lon_here * levels), BF16),
        ),
        in_specs=[vmem, hbm],
        out_specs=(vmem, vmem, vmem, vmem),
        scratch_shapes=[
            pltpu.VMEM((lon_here, lat_here, LANES), jnp.int32),
            pltpu.VMEM((lon_here, lat_here, LANES), F32),
            pltpu.VMEM((4, lon_here, levels, lat_here), F32),
            pltpu.VMEM((3, lat_here, lon_here * levels), F32),
            pltpu.SemaphoreType.DMA((lon_here // chunk,)),
        ],
        compiler_params=pltpu.CompilerParams(vmem_limit_bytes=40 << 20),
    )(rates, bits)


def unpack(packed, half):
    lane = lax.broadcasted_iota(jnp.int32, packed.shape, 1)
    first_half = lane % (2 * half) < half
    up = pltpu.roll(packed, half, 1)
    down = pltpu.roll(packed, LANES - half, 1)
    return jnp.where(first_half, packed, up), jnp.where(first_half, down, packed)


def compose(near, far):
    loss_a, cross_a, east_a, west_a = near
    loss_b, cross_b, east_b, west_b = far
    keep_a, keep_b = 1.0 - loss_a, 1.0 - loss_b
    return (
        loss_a + keep_a * loss_b,
        cross_a + keep_a * cross_b * keep_a,
        east_b + keep_b * east_a,
        west_a + keep_a * (west_b + cross_b * east_a),
    )


def exchange_kernel(
    inner,
    outer,
    lats,
    half,
    ends_ref,
    inside_hbm,
    coef_hbm,
    entry_ref,
    inside_halo,
    coef_halo,
    parts,
    joined,
    groups,
    solved,
    send_sem,
    recv_sem,
    halo_send,
    halo_recv,
):
    lon = lax.axis_index("lon")
    lat = lax.axis_index("lat")
    place, group = lon % inner, lon // inner
    lat_here = ends_ref.shape[1]
    rows = lat_here // inner
    top_half = inner // 2
    has_prev, has_next = lat > 0, lat < lats - 1
    prev_lat, next_lat = jnp.maximum(lat - 1, 0), jnp.minimum(lat + 1, lats - 1)

    def device(lon_id, lat_id):
        return {"lon": lon_id, "lat": lat_id}

    def mate(k):
        return (place + k) % inner

    def mate_lon(k):
        return group * inner + mate(k)

    def remote_lon(k):
        return (group + k) % outer * inner + place

    barrier = pltpu.get_barrier_semaphore()

    def greet(lon_id, lat_id):
        pl.semaphore_signal(barrier, inc=1, device_id=device(lon_id, lat_id), device_id_type=MESH)

    def greet_mates(k, _):
        greet(mate_lon(k), lat)
        return 0

    def greet_groups(k, _):
        greet(remote_lon(k), lat)
        return 0

    lax.fori_loop(1, inner, greet_mates, 0)
    lax.fori_loop(1, outer, greet_groups, 0)

    @pl.when(has_prev)
    def _():
        def greet_side(k, _):
            greet(group * inner + k, prev_lat)
            return 0

        lax.fori_loop(0, inner, greet_side, 0)

    @pl.when(has_next)
    def _():
        def greet_side(k, _):
            greet(group * inner + k, next_lat)
            return 0

        lax.fori_loop(0, inner, greet_side, 0)

    sides = has_prev.astype(jnp.int32) + has_next.astype(jnp.int32)
    pl.semaphore_wait(barrier, inner - 1 + outer - 1 + inner * sides)

    def part_rows(index):
        return pl.ds(pl.multiple_of(index * rows, rows), rows)

    def part_copy(k):
        return pltpu.make_async_remote_copy(
            src_ref=ends_ref.at[:, part_rows(mate(k)), :],
            dst_ref=parts.at[place],
            send_sem=send_sem.at[0, k],
            recv_sem=recv_sem.at[0, place],
            device_id=device(mate_lon(k), lat),
            device_id_type=MESH,
        )

    def part_arrival(k):
        return pltpu.make_async_remote_copy(
            src_ref=ends_ref.at[:, part_rows(mate(k)), :],
            dst_ref=parts.at[mate(k)],
            send_sem=send_sem.at[0, k],
            recv_sem=recv_sem.at[0, mate(k)],
            device_id=device(mate_lon(k), lat),
            device_id_type=MESH,
        )

    def send_part(k, _):
        part_copy(k).start()
        return 0

    lax.fori_loop(1, inner, send_part, 0)
    parts[place] = ends_ref[:, part_rows(place), :]

    def side_copies(first, slot, lat_id, base):
        return [
            pltpu.make_async_remote_copy(
                src_ref=inside_hbm.at[:, pl.ds(first, BAND), :],
                dst_ref=inside_halo.at[slot],
                send_sem=halo_send.at[base],
                recv_sem=halo_recv.at[slot * 2],
                device_id=device(lon, lat_id),
                device_id_type=MESH,
            ),
            pltpu.make_async_remote_copy(
                src_ref=coef_hbm.at[:, pl.ds(first, BAND), :],
                dst_ref=coef_halo.at[slot],
                send_sem=halo_send.at[base + 1],
                recv_sem=halo_recv.at[slot * 2 + 1],
                device_id=device(lon, lat_id),
                device_id_type=MESH,
            ),
        ]

    @pl.when(has_prev)
    def _():
        for copy in side_copies(0, 1, prev_lat, 0):
            copy.start()

    @pl.when(has_next)
    def _():
        for copy in side_copies(lat_here - BAND, 0, next_lat, 2):
            copy.start()

    def wait_part(k, _):
        part_arrival(k).wait_recv()
        return 0

    lax.fori_loop(1, inner, wait_part, 0)

    def map_of(ref, index):
        value = ref[index]
        loss, cross = unpack(value[2], half)
        return loss, cross, value[0], value[1]

    def join(p, near):
        return compose(near, map_of(parts, p))

    loss, cross, east, west = lax.fori_loop(1, inner, join, map_of(parts, 0))
    lane = lax.broadcasted_iota(jnp.int32, (rows, LANES), 1)
    packed = jnp.where(lane % (2 * half) < half, loss, cross)
    joined[0] = east
    joined[1] = west
    joined[2] = packed

    def group_copy(k):
        return pltpu.make_async_remote_copy(
            src_ref=joined,
            dst_ref=groups.at[group],
            send_sem=send_sem.at[1, k],
            recv_sem=recv_sem.at[1, group],
            device_id=device(remote_lon(k), lat),
            device_id_type=MESH,
        )

    def group_arrival(k):
        other = (group + k) % outer
        return pltpu.make_async_remote_copy(
            src_ref=joined,
            dst_ref=groups.at[other],
            send_sem=send_sem.at[1, k],
            recv_sem=recv_sem.at[1, other],
            device_id=device(remote_lon(k), lat),
            device_id_type=MESH,
        )

    def send_group(k, _):
        group_copy(k).start()
        return 0

    lax.fori_loop(1, outer, send_group, 0)
    groups[group, 0] = east
    groups[group, 1] = west
    groups[group, 2] = packed

    def wait_group(k, _):
        group_arrival(k).wait_recv()
        return 0

    lax.fori_loop(1, outer, wait_group, 0)

    zeros = jnp.zeros((rows, LANES), F32)

    def whole_east(z, carry):
        state, lost = carry
        loss_z, _, east_z, _ = map_of(groups, z)
        return east_z + state - loss_z * state, lost + loss_z - lost * loss_z

    end_state, lost = lax.fori_loop(0, outer, whole_east, (zeros, zeros))
    first_east = end_state / lost

    def whole_west(z, carry):
        state, kept, east_now = carry
        loss_z, cross_z, east_z, west_z = map_of(groups, z)
        keep_z = 1.0 - loss_z
        state = state + kept * (west_z + cross_z * east_now)
        return state, kept * keep_z, east_z + keep_z * east_now

    west_total, _, _ = lax.fori_loop(0, outer, whole_west, (zeros, zeros + 1.0, first_east))
    last_west = west_total / lost

    def to_group(z, state):
        loss_z, _, east_z, _ = map_of(groups, z)
        return east_z + state - loss_z * state

    east_here = lax.fori_loop(0, group, to_group, first_east)

    def west_before(z, carry):
        state, kept, east_now = carry
        loss_z, cross_z, east_z, west_z = map_of(groups, z)
        keep_z = 1.0 - loss_z
        state = state + kept * (west_z + cross_z * east_now)
        return state, kept * keep_z, east_z + keep_z * east_now

    _, _, east_after = lax.fori_loop(group, group + 1, west_before, (zeros, zeros + 1.0, east_here))
    state, kept, _ = lax.fori_loop(group + 1, outer, west_before, (zeros, zeros + 1.0, east_after))
    west_here = state + kept * last_west

    def inner_east(p, state):
        loss_p, _, east_p, _ = map_of(parts, p)
        solved[p, 0] = state
        return east_p + state - loss_p * state

    lax.fori_loop(0, inner, inner_east, east_here)

    def inner_west(k, state):
        p = inner - 1 - k
        loss_p, cross_p, _, west_p = map_of(parts, p)
        solved[p, 1] = state
        return west_p + cross_p * solved[p, 0] + state - loss_p * state

    lax.fori_loop(0, inner, inner_west, west_here)

    own_first = BAND

    def entry_rows(first):
        return pl.ds(pl.multiple_of(first, 8), rows)

    def entry_copy(k):
        return pltpu.make_async_remote_copy(
            src_ref=solved.at[mate(k)],
            dst_ref=entry_ref.at[:, entry_rows(own_first + place * rows), :],
            send_sem=send_sem.at[2, k],
            recv_sem=recv_sem.at[2, place],
            device_id=device(mate_lon(k), lat),
            device_id_type=MESH,
        )

    def entry_arrival(k):
        return pltpu.make_async_remote_copy(
            src_ref=solved.at[mate(k)],
            dst_ref=entry_ref.at[:, entry_rows(own_first + mate(k) * rows), :],
            send_sem=send_sem.at[2, k],
            recv_sem=recv_sem.at[2, mate(k)],
            device_id=device(mate_lon(k), lat),
            device_id_type=MESH,
        )

    def side_copy(p, first, lat_id):
        return pltpu.make_async_remote_copy(
            src_ref=solved.at[p],
            dst_ref=entry_ref.at[:, entry_rows(first), :],
            send_sem=send_sem.at[3, p],
            recv_sem=recv_sem.at[3, place],
            device_id=device(group * inner + p, lat_id),
            device_id_type=MESH,
        )

    def side_arrival(p, first):
        return pltpu.make_async_remote_copy(
            src_ref=solved.at[p],
            dst_ref=entry_ref.at[:, entry_rows(first), :],
            send_sem=send_sem.at[3, p],
            recv_sem=recv_sem.at[3, p],
            device_id=device(group * inner + p, lat),
            device_id_type=MESH,
        )

    below = own_first + lat_here

    def send_entry(k, _):
        entry_copy(k).start()
        return 0

    to_prev = jnp.logical_and(place < top_half, has_prev)
    to_next = jnp.logical_and(place >= top_half, has_next)
    prev_first = below + jnp.minimum(place, top_half - 1) * rows
    next_first = jnp.maximum(place - top_half, 0) * rows

    lax.fori_loop(1, inner, send_entry, 0)

    @pl.when(to_prev)
    def _():
        def send_side(p, _):
            side_copy(p, prev_first, prev_lat).start()
            return 0

        lax.fori_loop(0, inner, send_side, 0)

    @pl.when(to_next)
    def _():
        def send_side(p, _):
            side_copy(p, next_first, next_lat).start()
            return 0

        lax.fori_loop(0, inner, send_side, 0)

    entry_ref[:, entry_rows(own_first + place * rows), :] = solved[place]

    def wait_entry(k, _):
        entry_arrival(k).wait_recv()
        return 0

    lax.fori_loop(1, inner, wait_entry, 0)

    @pl.when(has_next)
    def _():
        def wait_side(p, _):
            side_arrival(p, below + p * rows).wait_recv()
            return 0

        lax.fori_loop(0, top_half, wait_side, 0)

    @pl.when(has_prev)
    def _():
        def wait_side(p, _):
            side_arrival(p, (p - top_half) * rows).wait_recv()
            return 0

        lax.fori_loop(top_half, inner, wait_side, 0)

    @pl.when(has_prev)
    def _():
        for copy in side_copies(0, 0, prev_lat, 0):
            copy.wait_recv()
        for copy in side_copies(0, 1, prev_lat, 0):
            copy.wait_send()

    @pl.when(has_next)
    def _():
        for copy in side_copies(lat_here - BAND, 1, next_lat, 2):
            copy.wait_recv()
        for copy in side_copies(lat_here - BAND, 0, next_lat, 2):
            copy.wait_send()

    def drain_inner(k, _):
        part_copy(k).wait_send()
        entry_copy(k).wait_send()
        return 0

    def drain_outer(k, _):
        group_copy(k).wait_send()
        return 0

    lax.fori_loop(1, inner, drain_inner, 0)
    lax.fori_loop(1, outer, drain_outer, 0)

    @pl.when(to_prev)
    def _():
        def drain(p, _):
            side_copy(p, prev_first, prev_lat).wait_send()
            return 0

        lax.fori_loop(0, inner, drain, 0)

    @pl.when(to_next)
    def _():
        def drain(p, _):
            side_copy(p, next_first, next_lat).wait_send()
            return 0

        lax.fori_loop(0, inner, drain, 0)


def run_exchange(mesh, levels, ends, inside, coef_small):
    lons, lats = mesh.shape["lon"], mesh.shape["lat"]
    inner = 8 if lons > 16 else 2
    outer = lons // inner
    _, lat_here, _ = ends.shape
    lon_here = inside.shape[0]
    rows = lat_here // inner
    half = LANES // levels // 2
    vmem = pl.BlockSpec(memory_space=pltpu.VMEM)
    hbm = pl.BlockSpec(memory_space=pl.ANY)
    most = max(inner, outer)
    return pl.pallas_call(
        functools.partial(exchange_kernel, inner, outer, lats, half),
        name="loop_exchange",
        out_shape=(
            jax.ShapeDtypeStruct((2, lat_here + 2 * BAND, LANES), F32),
            jax.ShapeDtypeStruct((2, lon_here, BAND, LANES), BF16),
            jax.ShapeDtypeStruct((2, 2, BAND, coef_small.shape[2]), BF16),
        ),
        in_specs=[vmem, hbm, hbm],
        out_specs=(vmem, hbm, hbm),
        scratch_shapes=[
            pltpu.VMEM((inner, 3, rows, LANES), F32),
            pltpu.VMEM((3, rows, LANES), F32),
            pltpu.VMEM((outer, 3, rows, LANES), F32),
            pltpu.VMEM((inner, 2, rows, LANES), F32),
            pltpu.SemaphoreType.DMA((4, most)),
            pltpu.SemaphoreType.DMA((4, most)),
            pltpu.SemaphoreType.DMA((4,)),
            pltpu.SemaphoreType.DMA((4,)),
        ],
        compiler_params=pltpu.CompilerParams(
            collective_id=0, has_side_effects=True, vmem_limit_bytes=16 << 20
        ),
    )(ends, inside, coef_small)


def combine_kernel(
    batch,
    levels,
    sides_ref,
    inside_ref,
    top_ref,
    bottom_ref,
    coef_ref,
    coef_top_ref,
    coef_bottom_ref,
    entry_ref,
    band_ref,
    level_ref,
    out_ref,
    zonal,
):
    columns_each = LANES // levels
    per_tile = LANES // levels
    lat_here = inside_ref.shape[1]
    below = BAND + lat_here
    first = pl.program_id(0) * batch % per_tile
    has_top, has_bottom = sides_ref[0] > 0, sides_ref[1] > 0

    def field(inside, coef, count, low, j):
        index = lane_index(count, (first + j) * levels, columns_each)
        east = entry_ref[0, pl.ds(low, count), :]
        west = entry_ref[1, pl.ds(low, count), :]
        cross = spread(coef[0].astype(F32), index)
        lost = spread(coef[1].astype(F32), index)
        return inside.astype(F32) + cross * east + (west - lost * west)

    zeros = jnp.zeros((BAND, LANES), F32)
    for pair in range(batch // 2):
        for side in range(2):
            j = 2 * pair + side
            lanes = pl.ds(side * LANES, LANES)
            upper = field(top_ref[0, j], coef_top_ref[0], BAND, 0, j)
            lower = field(bottom_ref[0, j], coef_bottom_ref[0], BAND, below, j)
            zonal[pair % 2, pl.ds(0, BAND), lanes] = jnp.where(has_top, upper, zeros).astype(BF16)
            zonal[pair % 2, pl.ds(BAND, lat_here), lanes] = field(
                inside_ref[j], coef_ref, lat_here, BAND, j
            ).astype(BF16)
            zonal[pair % 2, pl.ds(below, BAND), lanes] = jnp.where(
                has_bottom, lower, zeros
            ).astype(BF16)
        merid = jnp.dot(
            band_ref[...], zonal[pair % 2], preferred_element_type=F32
        ).astype(BF16)
        for side in range(2):
            out_ref[2 * pair + side] = jnp.dot(
                merid[:, side * LANES : (side + 1) * LANES],
                level_ref[...],
                preferred_element_type=F32,
            ).astype(BF16)


def run_combine(sides, inside, inside_halo, coef, coef_halo, entry, band_tile, level_map, levels):
    lon_here, lat_here, _ = inside.shape
    batch = 8
    per_tile = LANES // levels

    def tile_of(t):
        return t * batch // per_tile

    return pl.pallas_call(
        functools.partial(combine_kernel, batch, levels),
        name="band_product",
        grid=(lon_here // batch,),
        out_shape=jax.ShapeDtypeStruct((lon_here, lat_here, LANES), BF16),
        in_specs=[
            pl.BlockSpec(memory_space=pltpu.SMEM),
            pl.BlockSpec((batch, lat_here, LANES), lambda t: (t, 0, 0)),
            pl.BlockSpec((1, batch, BAND, LANES), lambda t: (0, t, 0, 0)),
            pl.BlockSpec((1, batch, BAND, LANES), lambda t: (1, t, 0, 0)),
            pl.BlockSpec((2, lat_here, LANES), lambda t: (0, 0, tile_of(t))),
            pl.BlockSpec((1, 2, BAND, LANES), lambda t: (0, 0, 0, tile_of(t))),
            pl.BlockSpec((1, 2, BAND, LANES), lambda t: (1, 0, 0, tile_of(t))),
            pl.BlockSpec((2, lat_here + 2 * BAND, LANES), lambda t: (0, 0, 0)),
            pl.BlockSpec(band_tile.shape, lambda t: (0, 0)),
            pl.BlockSpec(level_map.shape, lambda t: (0, 0)),
        ],
        out_specs=pl.BlockSpec((batch, lat_here, LANES), lambda t: (t, 0, 0)),
        scratch_shapes=[pltpu.VMEM((2, lat_here + 2 * BAND, 2 * LANES), BF16)],
        compiler_params=pltpu.CompilerParams(vmem_limit_bytes=24 << 20),
    )(
        sides,
        inside,
        inside_halo,
        inside_halo,
        coef,
        coef_halo,
        coef_halo,
        entry,
        band_tile,
        level_map,
    )


def solution(mesh):
    def per_device(sketch_bits, rates, merid_matrix, vert_matrix):
        lats = mesh.shape["lat"]
        levels = vert_matrix.shape[0]
        lat_here = sketch_bits.shape[1]
        lat = lax.axis_index("lat")
        padded_rows = jnp.pad(merid_matrix, ((0, 0), (BAND, BAND)))
        band_tile = lax.dynamic_slice_in_dim(
            padded_rows, lat * lat_here, lat_here + 2 * BAND, 1
        )
        ident_cols = jnp.eye(LANES // levels, dtype=BF16)
        level_map = (vert_matrix.T[:, None, :, None] * ident_cols[None, :, None, :]).reshape(
            LANES, LANES
        )
        sides = jnp.stack([lat > 0, lat < lats - 1]).astype(jnp.int32)
        ends, inside, coef, coef_small = run_filters(rates, sketch_bits)
        entry, inside_halo, coef_halo = run_exchange(mesh, levels, ends, inside, coef_small)
        return run_combine(
            sides, inside, inside_halo, coef, coef_halo, entry, band_tile, level_map, levels
        )

    in_specs = (P("lon", "lat", None), P("lon", None, "lat"), P("lat", None), P())
    out_specs = P("lon", "lat", None)
    return jax.shard_map(
        per_device, mesh=mesh, in_specs=in_specs, out_specs=out_specs, check_vma=False
    )
```

time: 747 us -> 65.7 us (0.09)
  blocking collectives: 272 us -> 0 us
  waiting for transfers between devices: 243 us -> 0 us
  local copies, waits for them, and re-layouts: 86.3 us -> 5.32 us
  Pallas kernels: 0 us -> 59.9 us
  other arithmetic: 53.8 us -> 0.17 us
  starting transfers between devices: 51.1 us -> 0 us
  matrix products: 26.7 us -> 0 us
  between operations: 13.8 us -> 0.04 us
    all_gather x2 -> x0, blocking collectives: 272 us -> none  [periodic_state(): lax.all_gather(own_pair[0][None], 'lon', axis=0, tiled=True)]
    all_gather x2 -> x0, waiting for transfers between devices: 228 us -> none  [periodic_state(): lax.all_gather(own_pair[1][None], 'lon', axis=0, tiled=True)]
    pallas_call x0 -> x3, Pallas kernels: none -> 59.9 us  [the longest x1 36.5 us: run_exchange(): pl.pallas_call(functools.partial(exchange_kernel, inner, outer, lats, hal...]
    ppermute x2 -> x0, starting transfers between devices: 51.1 us -> none  [the longest x1 49.2 us: with_halo(): lax.ppermute(tail, axis, [(i, (i + 1) % count) for i in range(ends)])]
    exp x12 -> x0, local copies, waits for them, and re-layouts: 30.5 us -> none  [the longest x6 14.1 us: within_slab(): decays = jnp.exp(-cum_chan)]
    dot_general x5 -> x0, matrix products: 26.7 us -> none  [the longest x2 19.6 us: within_slab(): jnp.dot(lower_mask, (source * jnp.exp(cum_chan)).reshape(rows_here, -1),...]
    another operation x2 -> x0, other arithmetic: 26.2 us -> none  [loop_entry(): cum_parts = jnp.cumsum(rate_parts, axis=0)]
    broadcast_in_dim x7 -> x0, local copies, waits for them, and re-layouts: 16.6 us -> none  [expand(): return jnp.repeat(per_level, chan_count // per_level.shape[-1], axis=-1)]
  transfers between devices with their start and end apart: 4 -> 0, of which waited for: 4 -> 0; matrix products, arithmetic and copies ran while one was open for 10% -> 0% of each run, Pallas kernels for 0% -> 0%
where the time goes in v1:
time: 65.7 us; the launch traced here: 65.5 us
  Pallas kernels  59.9 us (91%)
  local copies, waits for them, and re-layouts  5.32 us (8%)
    pallas_call x1, Pallas kernels, run_exchange(): pl.pallas_call(functools.partial(exchange_kernel, inner, outer, lats, hal...  36.5 us
    pallas_call x1, Pallas kernels, run_filters(): pl.pallas_call(functools.partial(filter_kernel, chunk), name='zonal_filte...  13.9 us
    pallas_call x1, Pallas kernels, run_combine(): pl.pallas_call(functools.partial(combine_kernel, batch, levels), name='ba...  9.52 us
    unnamed x4, local copies, waits for them, and re-layouts  3.33 us

profile of v1, /device:TPU:1, one launch (start us, length us, event | category | flops | bytes accessed | tf_op | source)
XLA Modules:
  0.0 65.5 jit_solution(13766264657239400294)
XLA Ops:
  0.0 0.1 add_convert_fusion.sides_ref
  0.1 0.8 %copy.5 = bf16[8,8]{1,0:T(8,128)(2,1)S(1)} copy(bf16[8,8]{0,1:T(8,128)(2,1)} %bitcast.5) | data formatting | bytes 256 | tf_op jit(solution)/shard_map/transpose | solution.py:697
  0.8 1.1 %pad_dynamic-slice_fusion.band_ref = bf16[192,384]{1,0:T(8,128)(2,1)S(1)} fusion(s32[]{:T(128)S(6)} %select_n.3, bf16[192,768]{1,0:T(8,128)(2,1)} %param.6), kind=kLoop, calls=%fused_computation | loop fusion | bytes 442372 | tf_op jit(solution)/shard_map/dynamic_slice | solution.py:693
  1.9 0.1 broadcast_multiply_fusion
  2.0 0.2 mul.24.level_ref
  2.2 0.0 copy-start
  2.2 2.3 %copy-done = s32[48,192,128]{2,1,0:T(8,128)S(1)} copy-done((s32[48,192,128]{2,1,0:T(8,128)S(1)}, s32[48,192,128]{2,1,0:T(8,128)}, u32[]{:S(2)}) %copy-start) | copy-done | bytes 4718616
  4.5 0.0 copy-start.1
  4.5 1.0 %copy-done.1 = f32[48,8,192]{2,1,0:T(8,128)S(1)} copy-done((f32[48,8,192]{2,1,0:T(8,128)S(1)}, f32[48,8,192]{2,1,0:T(8,128)}, u32[]{:S(2)}) %copy-start.1) | copy-done | bytes 294936
  5.5 13.9 %zonal_filters.1 = (f32[3,192,128]{2,1,0:T(8,128)S(1)}, bf16[48,192,128]{2,1,0:T(8,128)(2,1)S(1)}, f32[2,192,384]{2,1,0:T(8,128)S(1)}, bf16[2,192,384]{2,1,0:T(8,128)(2,1)S(1)}) custom-call(f32[48,8,192]{2,1,0:T(8,128)S(1)} %copy-done.1, s32[48,192,128]{2,1,0:T(8,128)S(1)} %copy-done), custom_call_target="tpu_custom_call" | custom-call | tf_op jit(solution)/shard_map/zonal_filters/pallas_call | solution.py:123
  19.5 36.5 %loop_exchange.1 = (f32[2,384,128]{2,1,0:T(8,128)S(1)}, bf16[2,48,96,128]{3,2,1,0:T(8,128)(2,1)S(1)}, bf16[2,2,96,384]{3,2,1,0:T(8,128)(2,1)S(1)}) custom-call(f32[3,192,128]{2,1,0:T(8,128)S(1)} %get-tuple-element.13.ends_ref, bf16[48,192,128]{2,1,0:T(8,128)(2,1)S(1)} %get-tuple-element.12.inside_hbm.inside_ref, ...), custom_call_target="tpu_custom_call" | custom-call | tf_op jit(solution)/shard_map/loop_exchange/pallas_call | solution.py:562
  55.9 9.5 %band_product.1 = bf16[48,192,128]{2,1,0:T(8,128)(2,1)} custom-call(s32[2]{0:T(128)S(1)} %add_convert_fusion.sides_ref, bf16[48,192,128]{2,1,0:T(8,128)(2,1)S(1)} %get-tuple-element.12.inside_hbm.inside_ref, bf16[2,48,96,128]{3,2,1,0:T(8,128)(2,1)S(1)} %get-tuple-element.15.top_ref.bottom_ref, ...), custom_call_target="tpu_custom_call" | custom-call | tf_op jit(solution)/shard_map/band_product/pallas_call | solution.py:652
  (1 shorter events, 0.0 us)
Async XLA Ops:
  2.2 2.3 %copy-start = (s32[48,192,128]{2,1,0:T(8,128)S(1)}, s32[48,192,128]{2,1,0:T(8,128)}, u32[]{:S(2)}) copy-start(s32[48,192,128]{2,1,0:T(8,128)} %bits_hbm.1) | copy-start | bytes 14155780
  4.5 1.0 %copy-start.1 = (f32[48,8,192]{2,1,0:T(8,128)S(1)}, f32[48,8,192]{2,1,0:T(8,128)}, u32[]{:S(2)}) copy-start(f32[48,8,192]{2,1,0:T(8,128)} %rates_ref.1) | copy-start | bytes 884740

commit v2 on v1

--- a/solution.py
+++ b/solution.py
@@ -15,9 +15,12 @@
 
 
 def loss_of(rate):
-    total = jnp.ones_like(rate)
-    for order in range(13, 1, -1):
-        total = 1.0 - total * rate * (1.0 / order)
+    factors = [1.0]
+    for order in range(2, 13):
+        factors.append(-factors[-1] / order)
+    total = jnp.full_like(rate, factors[-1])
+    for factor in reversed(factors[:-1]):
+        total = total * rate + factor
     return rate * total
 
 
@@ -31,115 +34,153 @@
 
 
 def filter_kernel(
-    chunk,
-    rates_ref,
+    block,
+    rates_hbm,
     bits_hbm,
     ends_ref,
     inside_ref,
     coef_ref,
     coef_small_ref,
+    rates_ref,
     bits,
     east,
+    decay_chan,
     lev_scratch,
     lat_scratch,
+    total,
     sems,
 ):
     lon_here, levels, lat_here = rates_ref.shape
     columns_each = LANES // levels
     per_tile = LANES // levels
-    steps = lon_here // chunk
+    tiles = lon_here // per_tile
+    blocks = lat_here // block
+    rates_copy = pltpu.make_async_copy(rates_hbm, rates_ref, sems.at[tiles])
+    rates_copy.start()
     copies = [
         pltpu.make_async_copy(
-            bits_hbm.at[pl.ds(t * chunk, chunk)], bits.at[pl.ds(t * chunk, chunk)], sems.at[t]
-        )
-        for t in range(steps)
+            bits_hbm.at[pl.ds(t * per_tile, per_tile)],
+            bits.at[pl.ds(t * per_tile, per_tile)],
+            sems.at[t],
+        )
+        for t in range(tiles)
     ]
     for copy in copies:
         copy.start()
+    rates_copy.wait()
 
     loss = loss_of(rates_ref[...])
     squared = loss * (2.0 - loss)
     decay = 1.0 - loss
-    lev_scratch[0] = loss
-    lev_scratch[1] = squared / jnp.sqrt(1.0 + decay * decay)
-    lat_scratch[0] = loss.reshape(lon_here * levels, lat_here).T
+    gain_out = squared * lax.rsqrt(1.0 + decay * decay)
+    lev_scratch[0] = decay
+    lev_scratch[1] = gain_out
+    lev_scratch[4] = loss
+    lat_scratch[0] = decay.reshape(lon_here * levels, lat_here).T
     lat_scratch[1] = jnp.sqrt(squared).reshape(lon_here * levels, lat_here).T
-    lat_scratch[2] = lev_scratch[1].reshape(lon_here * levels, lat_here).T
+    lat_scratch[2] = gain_out.reshape(lon_here * levels, lat_here).T
 
     passed = jnp.ones((levels, lat_here), F32)
+    lost = jnp.zeros((levels, lat_here), F32)
     for i in range(lon_here):
-        passed = passed - lev_scratch[0, i] * passed
+        passed = lev_scratch[0, i] * passed
+        lost = lost + lev_scratch[4, i] * (1.0 - lost)
         lev_scratch[2, i] = passed
     coef = jnp.zeros((levels, lat_here), F32)
-    lost = jnp.zeros((levels, lat_here), F32)
+    kept = jnp.ones((levels, lat_here), F32)
     for i in reversed(range(lon_here)):
         here = lev_scratch[0, i]
-        coef = coef - here * coef + lev_scratch[1, i] * lev_scratch[2, i]
-        lost = lost + (here - here * lost)
+        coef = here * coef + lev_scratch[1, i] * lev_scratch[2, i]
+        kept = here * kept
         lev_scratch[2, i] = coef
-        lev_scratch[3, i] = lost
+        lev_scratch[3, i] = kept
     coef_ref[0] = lev_scratch[2].reshape(lon_here * levels, lat_here).T
     coef_ref[1] = lev_scratch[3].reshape(lon_here * levels, lat_here).T
     coef_small_ref[...] = coef_ref[...].astype(BF16)
-
-    def expanded(which, i):
-        column = pl.multiple_of(i // per_tile * LANES, LANES)
-        index = lane_index(lat_here, i % per_tile * levels, columns_each)
-        return spread(lat_scratch[which, :, pl.ds(column, LANES)], index)
-
-    def forward(i, state):
-        gain = expanded(1, i)
-        state = state - expanded(0, i) * state + jnp.where(bits[i] > 0, gain, -gain)
-        east[i] = state
-        return state
-
-    def backward(k, state):
-        i = lon_here - 1 - k
-        state = state - expanded(0, i) * state + expanded(2, i) * east[i]
-        inside_ref[i] = state.astype(BF16)
-        return state
-
-    state = jnp.zeros((lat_here, LANES), F32)
-    for t in range(steps):
+    total[:, :levels] = lost.T
+
+    def rows_of(b):
+        return pl.ds(pl.multiple_of(b * block, block), block)
+
+    ends_ref[0] = jnp.zeros((lat_here, LANES), F32)
+    ends_ref[1] = jnp.zeros((lat_here, LANES), F32)
+    for t in range(tiles):
         copies[t].wait()
-        state = lax.fori_loop(t * chunk, (t + 1) * chunk, forward, state)
-    ends_ref[0] = state
-    ends_ref[1] = lax.fori_loop(0, lon_here, backward, jnp.zeros_like(state))
+        lanes = pl.ds(t * LANES, LANES)
+
+        def forward(b, _):
+            rows = rows_of(b)
+            decays, gains = lat_scratch[0, rows, lanes], lat_scratch[1, rows, lanes]
+            state = ends_ref[0, rows, :]
+            for j in range(per_tile):
+                i = t * per_tile + j
+                index = lane_index(block, j * levels, columns_each)
+                gain = spread(gains, index)
+                decay = spread(decays, index)
+                decay_chan[i, rows, :] = decay
+                state = decay * state + jnp.where(bits[i, rows, :] > 0, gain, -gain)
+                east[i, rows, :] = state
+            ends_ref[0, rows, :] = state
+            return 0
+
+        lax.fori_loop(0, blocks, forward, 0)
+
+    for t in reversed(range(tiles)):
+        lanes = pl.ds(t * LANES, LANES)
+
+        def backward(b, _):
+            rows = rows_of(b)
+            gains = lat_scratch[2, rows, lanes]
+            state = ends_ref[1, rows, :]
+            for j in reversed(range(per_tile)):
+                i = t * per_tile + j
+                index = lane_index(block, j * levels, columns_each)
+                state = decay_chan[i, rows, :] * state + spread(gains, index) * east[i, rows, :]
+                inside_ref[i, rows, :] = state.astype(BF16)
+            ends_ref[1, rows, :] = state
+            return 0
+
+        lax.fori_loop(0, blocks, backward, 0)
+
     index = lane_index(lat_here, 0, columns_each)
     lane = lax.broadcasted_iota(jnp.int32, (lat_here, LANES), 1)
     first_half = lane % columns_each < columns_each // 2
     ends_ref[2] = jnp.where(
-        first_half,
-        spread(coef_ref[1, :, :LANES], index),
-        spread(coef_ref[0, :, :LANES], index),
+        first_half, spread(total[...], index), spread(coef_ref[0, :, :LANES], index)
     )
 
 
 def run_filters(rates, bits):
     lon_here, levels, lat_here = rates.shape
-    chunk = 8
     vmem = pl.BlockSpec(memory_space=pltpu.VMEM)
     hbm = pl.BlockSpec(memory_space=pltpu.HBM)
+    columns = lon_here * levels
     return pl.pallas_call(
-        functools.partial(filter_kernel, chunk),
+        functools.partial(filter_kernel, 64),
         name="zonal_filters",
         out_shape=(
             jax.ShapeDtypeStruct((3, lat_here, LANES), F32),
             jax.ShapeDtypeStruct((lon_here, lat_here, LANES), BF16),
-            jax.ShapeDtypeStruct((2, lat_here, lon_here * levels), F32),
-            jax.ShapeDtypeStruct((2, lat_here, lon_here * levels), BF16),
+            jax.ShapeDtypeStruct((2, lat_here, columns), F32),
+            jax.ShapeDtypeStruct((2, lat_here, columns), BF16),
         ),
-        in_specs=[vmem, hbm],
+        in_specs=[hbm, hbm],
         out_specs=(vmem, vmem, vmem, vmem),
         scratch_shapes=[
+            pltpu.VMEM((lon_here, levels, lat_here), F32),
             pltpu.VMEM((lon_here, lat_here, LANES), jnp.int32),
             pltpu.VMEM((lon_here, lat_here, LANES), F32),
-            pltpu.VMEM((4, lon_here, levels, lat_here), F32),
-            pltpu.VMEM((3, lat_here, lon_here * levels), F32),
-            pltpu.SemaphoreType.DMA((lon_here // chunk,)),
+            pltpu.VMEM((lon_here, lat_here, LANES), F32),
+            pltpu.VMEM((5, lon_here, levels, lat_here), F32),
+            pltpu.VMEM((3, lat_here, columns), F32),
+            pltpu.VMEM((lat_here, LANES), F32),
+            pltpu.SemaphoreType.DMA((columns // LANES + 1,)),
         ],
         compiler_params=pltpu.CompilerParams(vmem_limit_bytes=40 << 20),
-    )(rates, bits)
+    )(
+        pltpu.with_memory_space_constraint(rates, pltpu.HBM),
+        pltpu.with_memory_space_constraint(bits, pltpu.HBM),
+    )
 
 
 def unpack(packed, half):
@@ -170,9 +211,14 @@
     ends_ref,
     inside_hbm,
     coef_hbm,
+    merid_ref,
+    vert_ref,
     entry_ref,
     inside_halo,
     coef_halo,
+    band_ref,
+    level_ref,
+    coef_landing,
     parts,
     joined,
     groups,
@@ -235,6 +281,42 @@
 
         lax.fori_loop(0, inner, greet_side, 0)
 
+    lat_all = merid_ref.shape[1]
+    spans = (lat_all, lat_here + 2 * BAND)
+    source = lax.broadcasted_iota(jnp.int32, spans, 0)
+    target = lax.broadcasted_iota(jnp.int32, spans, 1)
+    pick = jnp.where(source - target == lat * lat_here - BAND, 1.0, 0.0).astype(BF16)
+    band_ref[...] = jnp.dot(merid_ref[...], pick, preferred_element_type=F32).astype(BF16)
+    levels = vert_ref.shape[0]
+    columns_each = LANES // levels
+    column = lax.broadcasted_iota(jnp.int32, (LANES, levels), 0)
+    level = lax.broadcasted_iota(jnp.int32, (LANES, levels), 1)
+    member = jnp.where(column // columns_each == level, 1.0, 0.0).astype(BF16)
+    along = (((1,), (1,)), ((), ()))
+    by_row = lax.dot_general(member, vert_ref[...], along, preferred_element_type=F32)
+    full = lax.dot_general(by_row.astype(BF16), member, along, preferred_element_type=F32)
+    row = lax.broadcasted_iota(jnp.int32, (LANES, LANES), 0)
+    col = lax.broadcasted_iota(jnp.int32, (LANES, LANES), 1)
+    same = row % columns_each == col % columns_each
+    level_ref[...] = jnp.where(same, full, 0.0).astype(BF16)
+
+    def clear(slot, first):
+        def clear_lon(i, _):
+            inside_halo[slot, i] = jnp.zeros(inside_halo.shape[2:], BF16)
+            return 0
+
+        lax.fori_loop(0, inside_halo.shape[1], clear_lon, 0)
+        coef_halo[slot] = jnp.zeros(coef_halo.shape[1:], F32)
+        entry_ref[:, pl.ds(first, BAND), :] = jnp.zeros((2, BAND, LANES), F32)
+
+    @pl.when(jnp.logical_not(has_prev))
+    def _():
+        clear(0, 0)
+
+    @pl.when(jnp.logical_not(has_next))
+    def _():
+        clear(1, BAND + lat_here)
+
     sides = has_prev.astype(jnp.int32) + has_next.astype(jnp.int32)
     pl.semaphore_wait(barrier, inner - 1 + outer - 1 + inner * sides)
 
@@ -280,7 +362,7 @@
             ),
             pltpu.make_async_remote_copy(
                 src_ref=coef_hbm.at[:, pl.ds(first, BAND), :],
-                dst_ref=coef_halo.at[slot],
+                dst_ref=coef_landing.at[slot],
                 send_sem=halo_send.at[base + 1],
                 recv_sem=halo_recv.at[slot * 2 + 1],
                 device_id=device(lon, lat_id),
@@ -507,15 +589,19 @@
 
     @pl.when(has_prev)
     def _():
-        for copy in side_copies(0, 0, prev_lat, 0):
-            copy.wait_recv()
+        inside_copy, coef_copy = side_copies(0, 0, prev_lat, 0)
+        coef_copy.wait_recv()
+        coef_halo[0] = coef_landing[0].astype(F32)
+        inside_copy.wait_recv()
         for copy in side_copies(0, 1, prev_lat, 0):
             copy.wait_send()
 
     @pl.when(has_next)
     def _():
-        for copy in side_copies(lat_here - BAND, 1, next_lat, 2):
-            copy.wait_recv()
+        inside_copy, coef_copy = side_copies(lat_here - BAND, 1, next_lat, 2)
+        coef_copy.wait_recv()
+        coef_halo[1] = coef_landing[1].astype(F32)
+        inside_copy.wait_recv()
         for copy in side_copies(lat_here - BAND, 0, next_lat, 2):
             copy.wait_send()
 
@@ -548,7 +634,7 @@
         lax.fori_loop(0, inner, drain, 0)
 
 
-def run_exchange(mesh, levels, ends, inside, coef_small):
+def run_exchange(mesh, levels, ends, inside, coef_small, merid, vert):
     lons, lats = mesh.shape["lon"], mesh.shape["lat"]
     inner = 8 if lons > 16 else 2
     outer = lons // inner
@@ -565,11 +651,14 @@
         out_shape=(
             jax.ShapeDtypeStruct((2, lat_here + 2 * BAND, LANES), F32),
             jax.ShapeDtypeStruct((2, lon_here, BAND, LANES), BF16),
-            jax.ShapeDtypeStruct((2, 2, BAND, coef_small.shape[2]), BF16),
+            jax.ShapeDtypeStruct((2, 2, BAND, coef_small.shape[2]), F32),
+            jax.ShapeDtypeStruct((lat_here, lat_here + 2 * BAND), BF16),
+            jax.ShapeDtypeStruct((LANES, LANES), BF16),
         ),
-        in_specs=[vmem, hbm, hbm],
-        out_specs=(vmem, hbm, hbm),
+        in_specs=[vmem, hbm, hbm, vmem, vmem],
+        out_specs=(vmem, vmem, vmem, vmem, vmem),
         scratch_shapes=[
+            pltpu.VMEM((2, 2, BAND, coef_small.shape[2]), BF16),
             pltpu.VMEM((inner, 3, rows, LANES), F32),
             pltpu.VMEM((3, rows, LANES), F32),
             pltpu.VMEM((outer, 3, rows, LANES), F32),
@@ -582,13 +671,12 @@
         compiler_params=pltpu.CompilerParams(
             collective_id=0, has_side_effects=True, vmem_limit_bytes=16 << 20
         ),
-    )(ends, inside, coef_small)
+    )(ends, inside, coef_small, merid, vert)
 
 
 def combine_kernel(
     batch,
     levels,
-    sides_ref,
     inside_ref,
     top_ref,
     bottom_ref,
@@ -606,33 +694,25 @@
     lat_here = inside_ref.shape[1]
     below = BAND + lat_here
     first = pl.program_id(0) * batch % per_tile
-    has_top, has_bottom = sides_ref[0] > 0, sides_ref[1] > 0
 
     def field(inside, coef, count, low, j):
         index = lane_index(count, (first + j) * levels, columns_each)
-        east = entry_ref[0, pl.ds(low, count), :]
-        west = entry_ref[1, pl.ds(low, count), :]
-        cross = spread(coef[0].astype(F32), index)
-        lost = spread(coef[1].astype(F32), index)
-        return inside.astype(F32) + cross * east + (west - lost * west)
-
-    zeros = jnp.zeros((BAND, LANES), F32)
+        rows = pl.ds(low, count)
+        east = spread(coef[0], index) * entry_ref[0, rows, :]
+        west = spread(coef[1], index) * entry_ref[1, rows, :]
+        return (inside.astype(F32) + east + west).astype(BF16)
+
     for pair in range(batch // 2):
+        held = zonal.at[pair % 2]
         for side in range(2):
             j = 2 * pair + side
             lanes = pl.ds(side * LANES, LANES)
-            upper = field(top_ref[0, j], coef_top_ref[0], BAND, 0, j)
-            lower = field(bottom_ref[0, j], coef_bottom_ref[0], BAND, below, j)
-            zonal[pair % 2, pl.ds(0, BAND), lanes] = jnp.where(has_top, upper, zeros).astype(BF16)
-            zonal[pair % 2, pl.ds(BAND, lat_here), lanes] = field(
-                inside_ref[j], coef_ref, lat_here, BAND, j
-            ).astype(BF16)
-            zonal[pair % 2, pl.ds(below, BAND), lanes] = jnp.where(
-                has_bottom, lower, zeros
-            ).astype(BF16)
-        merid = jnp.dot(
-            band_ref[...], zonal[pair % 2], preferred_element_type=F32
-        ).astype(BF16)
+            held[pl.ds(0, BAND), lanes] = field(top_ref[0, j], coef_top_ref[0], BAND, 0, j)
+            held[pl.ds(BAND, lat_here), lanes] = field(inside_ref[j], coef_ref, lat_here, BAND, j)
+            held[pl.ds(below, BAND), lanes] = field(
+                bottom_ref[0, j], coef_bottom_ref[0], BAND, below, j
+            )
+        merid = jnp.dot(band_ref[...], held[...], preferred_element_type=F32).astype(BF16)
         for side in range(2):
             out_ref[2 * pair + side] = jnp.dot(
                 merid[:, side * LANES : (side + 1) * LANES],
@@ -641,7 +721,7 @@
             ).astype(BF16)
 
 
-def run_combine(sides, inside, inside_halo, coef, coef_halo, entry, band_tile, level_map, levels):
+def run_combine(inside, inside_halo, coef, coef_halo, entry, band_tile, level_map, levels):
     lon_here, lat_here, _ = inside.shape
     batch = 8
     per_tile = LANES // levels
@@ -655,7 +735,6 @@
         grid=(lon_here // batch,),
         out_shape=jax.ShapeDtypeStruct((lon_here, lat_here, LANES), BF16),
         in_specs=[
-            pl.BlockSpec(memory_space=pltpu.SMEM),
             pl.BlockSpec((batch, lat_here, LANES), lambda t: (t, 0, 0)),
             pl.BlockSpec((1, batch, BAND, LANES), lambda t: (0, t, 0, 0)),
             pl.BlockSpec((1, batch, BAND, LANES), lambda t: (1, t, 0, 0)),
@@ -669,39 +748,18 @@
         out_specs=pl.BlockSpec((batch, lat_here, LANES), lambda t: (t, 0, 0)),
         scratch_shapes=[pltpu.VMEM((2, lat_here + 2 * BAND, 2 * LANES), BF16)],
         compiler_params=pltpu.CompilerParams(vmem_limit_bytes=24 << 20),
-    )(
-        sides,
-        inside,
-        inside_halo,
-        inside_halo,
-        coef,
-        coef_halo,
-        coef_halo,
-        entry,
-        band_tile,
-        level_map,
-    )
+    )(inside, inside_halo, inside_halo, coef, coef_halo, coef_halo, entry, band_tile, level_map)
 
 
 def solution(mesh):
     def per_device(sketch_bits, rates, merid_matrix, vert_matrix):
-        lats = mesh.shape["lat"]
         levels = vert_matrix.shape[0]
-        lat_here = sketch_bits.shape[1]
-        lat = lax.axis_index("lat")
-        padded_rows = jnp.pad(merid_matrix, ((0, 0), (BAND, BAND)))
-        band_tile = lax.dynamic_slice_in_dim(
-            padded_rows, lat * lat_here, lat_here + 2 * BAND, 1
-        )
-        ident_cols = jnp.eye(LANES // levels, dtype=BF16)
-        level_map = (vert_matrix.T[:, None, :, None] * ident_cols[None, :, None, :]).reshape(
-            LANES, LANES
-        )
-        sides = jnp.stack([lat > 0, lat < lats - 1]).astype(jnp.int32)
         ends, inside, coef, coef_small = run_filters(rates, sketch_bits)
-        entry, inside_halo, coef_halo = run_exchange(mesh, levels, ends, inside, coef_small)
+        entry, inside_halo, coef_halo, band_tile, level_map = run_exchange(
+            mesh, levels, ends, inside, coef_small, merid_matrix, vert_matrix
+        )
         return run_combine(
-            sides, inside, inside_halo, coef, coef_halo, entry, band_tile, level_map, levels
+            inside, inside_halo, coef, coef_halo, entry, band_tile, level_map, levels
         )
 
     in_specs = (P("lon", "lat", None), P("lon", None, "lat"), P("lat", None), P())

time: 65.7 us -> 55.9 us (0.85)
  local copies, waits for them, and re-layouts: 5.32 us -> 0.01 us
  Pallas kernels: 59.9 us -> 55.8 us
    pallas_call x1, Pallas kernels: 13.9 us -> 8.02 us  [run_filters(): pl.pallas_call(functools.partial(filter_kernel, 64), name='zonal_filters'...]
    unnamed x4, local copies, waits for them, and re-layouts: 3.33 us -> 0.01 us
    pallas_call x1, Pallas kernels: 9.52 us -> 11.3 us  [run_combine(): pl.pallas_call(functools.partial(combine_kernel, batch, levels), name='ba...]
    dynamic_slice x1 -> x0, local copies, waits for them, and re-layouts: 1.05 us -> none  [per_device(): lax.dynamic_slice_in_dim(padded_rows, lat * lat_here, lat_here + 2 * BAND...]
    transpose x1 -> x0, local copies, waits for them, and re-layouts: 0.76 us -> none  [per_device(): vert_matrix.T[:, None, :, None] * ident_cols[None, :, None, :]]
where the time goes in v2:
time: 55.9 us
  Pallas kernels  55.8 us (100%)
    pallas_call x1, Pallas kernels, run_exchange(): pl.pallas_call(functools.partial(exchange_kernel, inner, outer, lats, hal...  36.5 us
    pallas_call x1, Pallas kernels, run_combine(): pl.pallas_call(functools.partial(combine_kernel, batch, levels), name='ba...  11.3 us
    pallas_call x1, Pallas kernels, run_filters(): pl.pallas_call(functools.partial(filter_kernel, 64), name='zonal_filters'...  8.02 us

profile of v2, /device:TPU:1, one launch (start us, length us, event | category | flops | bytes accessed | tf_op | source)
XLA Modules:
  0.0 55.9 jit_solution(14100560660262215146)
XLA Ops:
  0.0 0.0 copy-start.1
  0.0 0.0 copy-start
  0.0 8.0 %zonal_filters.1 = (f32[3,192,128]{2,1,0:T(8,128)S(1)}, bf16[48,192,128]{2,1,0:T(8,128)(2,1)S(1)}, f32[2,192,384]{2,1,0:T(8,128)S(1)}, bf16[2,192,384]{2,1,0:T(8,128)(2,1)S(1)}) custom-call(f32[48,8,192]{2,1,0:T(8,128)} %rates_hbm.1, s32[48,192,128]{2,1,0:T(8,128)} %bits_hbm.1), custom_call_target="tpu_custom_call" | custom-call | tf_op jit(solution)/shard_map/zonal_filters/pallas_call | solution.py:158
  8.0 0.0 copy-done.1
  8.0 0.0 copy-done
  8.1 36.5 %loop_exchange.1 = (f32[2,384,128]{2,1,0:T(8,128)S(1)}, bf16[2,48,96,128]{3,2,1,0:T(8,128)(2,1)S(1)}, f32[2,2,96,384]{3,2,1,0:T(8,128)S(1)}, bf16[192,384]{1,0:T(8,128)(2,1)S(1)}, bf16[128,128]{1,0:T(8,128)(2,1)S(1)}) custom-call(f32[3,192,128]{2,1,0:T(8,128)S(1)} %get-tuple-element.15.ends_ref, ...), custom_call_target="tpu_custom_call" | custom-call | tf_op jit(solution)/shard_map/loop_exchange/pallas_call | solution.py:648
  44.6 11.3 %band_product.1 = bf16[48,192,128]{2,1,0:T(8,128)(2,1)} custom-call(bf16[48,192,128]{2,1,0:T(8,128)(2,1)S(1)} %get-tuple-element.14.inside_hbm.inside_ref, bf16[2,48,96,128]{3,2,1,0:T(8,128)(2,1)S(1)} %get-tuple-element.17.top_ref.bottom_ref, bf16[2,48,96,128]{3,2,1,0:T(8,128)(2,1)S(1)} %get-tuple-element.17.top_ref.bottom_ref, ...), custom_call_target="tpu_custom_call" | custom-call | tf_op jit(solution)/shard_map/band_product/pallas_call | solution.py:732
Async XLA Ops:
  0.0 8.0 %copy-start.1 = (bf16[8,8]{1,0:T(8,128)(2,1)S(1)}, bf16[8,8]{1,0:T(8,128)(2,1)}, u32[]{:S(2)}) copy-start(bf16[8,8]{1,0:T(8,128)(2,1)} %vert_ref.1) | copy-start | bytes 388
  0.0 8.0 %copy-start = (bf16[192,768]{1,0:T(8,128)(2,1)S(1)}, bf16[192,768]{1,0:T(8,128)(2,1)}, u32[]{:S(2)}) copy-start(bf16[192,768]{1,0:T(8,128)(2,1)} %merid_ref.1) | copy-start | bytes 884740

commit v3 on v2

v3 whole, which is shorter than its diff:
```python
import functools

import jax
import jax.numpy as jnp
from jax import lax
from jax.experimental import pallas as pl
from jax.experimental.pallas import tpu as pltpu
from jax.sharding import PartitionSpec as P

BAND = 96
LANES = 128
F32 = jnp.float32
BF16 = jnp.bfloat16
MESH = pl.DeviceIdType.MESH


def loss_of(rate):
    factors = [1.0]
    for order in range(2, 13):
        factors.append(-factors[-1] / order)
    total = jnp.full_like(rate, factors[-1])
    for factor in reversed(factors[:-1]):
        total = total * rate + factor
    return rate * total


def filter_kernel(
    rates_hbm,
    bits_hbm,
    ends_ref,
    inside_ref,
    inside_small_ref,
    coef_ref,
    coef_small_ref,
    rates_ref,
    bits,
    even,
    odd,
    state_ref,
    lev,
    sems,
):
    lon_here, levels, lat_here = rates_ref.shape
    each = LANES // levels
    width = 2 * LANES
    second = lat_here - LANES
    rates_copy = pltpu.make_async_copy(rates_hbm, rates_ref, sems.at[0])
    bits_copy = pltpu.make_async_copy(bits_hbm, bits, sems.at[1])
    rates_copy.start()
    bits_copy.start()
    rates_copy.wait()

    rate = jnp.concatenate([rates_ref[:, :, :LANES], rates_ref[:, :, second:]], axis=2)
    loss = loss_of(rate)
    squared = loss * (2.0 - loss)
    decay = 1.0 - loss
    lev[0] = decay
    lev[1] = jnp.sqrt(squared)
    lev[2] = squared * lax.rsqrt(1.0 + decay * decay)
    lev[3] = loss

    passed = jnp.ones((levels, width), F32)
    lost = jnp.zeros((levels, width), F32)
    for i in range(lon_here):
        passed = lev[0, i] * passed
        lost = lost + lev[3, i] * (1.0 - lost)
        coef_ref[0, i] = passed
    coef = jnp.zeros((levels, width), F32)
    kept = jnp.ones((levels, width), F32)
    for i in reversed(range(lon_here)):
        here = lev[0, i]
        coef = here * coef + lev[2, i] * coef_ref[0, i]
        kept = here * kept
        coef_ref[0, i] = coef
        coef_ref[1, i] = kept
    for which in range(2):
        coef_small_ref[which] = coef_ref[which].reshape(lon_here * levels, width).astype(BF16)

    def part(level):
        return pl.ds(level * each, each)

    def wide(which, i, level):
        return jnp.broadcast_to(lev[which, i, pl.ds(level, 1), :], (each, width))

    def turn(i, ref):
        ref[:, :LANES] = bits[i, :LANES, :].T
        ref[:, LANES:] = bits[i, second:, :].T

    def forward(i, turned):
        for level in range(levels):
            gain = wide(1, i, level)
            state = wide(0, i, level) * state_ref[part(level), :]
            state = state + jnp.where(turned[part(level), :] > 0, gain, -gain)
            inside_ref[i, part(level), :] = state
            state_ref[part(level), :] = state

    def backward(i):
        for level in range(levels):
            state = wide(0, i, level) * state_ref[part(level), :]
            state = state + wide(2, i, level) * inside_ref[i, part(level), :]
            inside_ref[i, part(level), :] = state
            inside_small_ref[i, part(level), :] = state.astype(BF16)
            state_ref[part(level), :] = state

    def put_ends(first):
        for level in range(levels):
            ends_ref[level, pl.ds(first, each), :] = state_ref[part(level), :]

    bits_copy.wait()
    state_ref[...] = jnp.zeros(state_ref.shape, F32)
    turn(0, even)

    def go_east(k, _):
        turn(2 * k + 1, odd)
        forward(2 * k, even)
        turn(jnp.minimum(2 * k + 2, lon_here - 1), even)
        forward(2 * k + 1, odd)
        return 0

    lax.fori_loop(0, lon_here // 2, go_east, 0)
    put_ends(0)
    state_ref[...] = jnp.zeros(state_ref.shape, F32)

    def go_west(k, _):
        backward(lon_here - 1 - 2 * k)
        backward(lon_here - 2 - 2 * k)
        return 0

    lax.fori_loop(0, lon_here // 2, go_west, 0)
    put_ends(each)
    for level in range(levels):
        ends_ref[level, pl.ds(2 * each, 8), :] = jnp.concatenate(
            [lost[level : level + 1], coef[level : level + 1], jnp.zeros((6, width), F32)], axis=0
        )


def run_filters(rates, bits):
    lon_here, levels, lat_here = rates.shape
    vmem = pl.BlockSpec(memory_space=pltpu.VMEM)
    hbm = pl.BlockSpec(memory_space=pltpu.HBM)
    width = 2 * LANES
    return pl.pallas_call(
        filter_kernel,
        name="zonal_filters",
        out_shape=(
            jax.ShapeDtypeStruct((levels, 2 * LANES // levels + 8, width), F32),
            jax.ShapeDtypeStruct((lon_here, LANES, width), F32),
            jax.ShapeDtypeStruct((lon_here, LANES, width), BF16),
            jax.ShapeDtypeStruct((2, lon_here, levels, width), F32),
            jax.ShapeDtypeStruct((2, lon_here * levels, width), BF16),
        ),
        in_specs=[hbm, hbm],
        out_specs=(vmem,) * 5,
        scratch_shapes=[
            pltpu.VMEM((lon_here, levels, lat_here), F32),
            pltpu.VMEM((lon_here, lat_here, LANES), jnp.int32),
            pltpu.VMEM((LANES, width), jnp.int32),
            pltpu.VMEM((LANES, width), jnp.int32),
            pltpu.VMEM((LANES, width), F32),
            pltpu.VMEM((4, lon_here, levels, width), F32),
            pltpu.SemaphoreType.DMA((2,)),
        ],
        compiler_params=pltpu.CompilerParams(vmem_limit_bytes=32 << 20),
    )(
        pltpu.with_memory_space_constraint(rates, pltpu.HBM),
        pltpu.with_memory_space_constraint(bits, pltpu.HBM),
    )


def compose(near, far):
    loss_a, cross_a, east_a, west_a = near
    loss_b, cross_b, east_b, west_b = far
    keep_a, keep_b = 1.0 - loss_a, 1.0 - loss_b
    return (
        loss_a + keep_a * loss_b,
        cross_a + keep_a * cross_b * keep_a,
        east_b + keep_b * east_a,
        west_a + keep_a * (west_b + cross_b * east_a),
    )


def exchange_kernel(
    inner,
    outer,
    lats,
    ends_ref,
    inside_hbm,
    coef_hbm,
    merid_ref,
    vert_ref,
    entry_ref,
    inside_halo,
    coef_halo,
    band_ref,
    level_ref,
    coef_landing,
    parts,
    joined,
    groups,
    solved,
    send_sem,
    recv_sem,
    halo_send,
    halo_recv,
):
    lon = lax.axis_index("lon")
    lat = lax.axis_index("lat")
    place, group = lon % inner, lon // inner
    lat_here = band_ref.shape[0]
    each = LANES // inner
    has_prev, has_next = lat > 0, lat < lats - 1
    prev_lat, next_lat = jnp.maximum(lat - 1, 0), jnp.minimum(lat + 1, lats - 1)

    def device(lon_id, lat_id):
        return {"lon": lon_id, "lat": lat_id}

    def mate(k):
        return (place + k) % inner

    def mate_lon(k):
        return group * inner + mate(k)

    def remote_lon(k):
        return (group + k) % outer * inner + place

    barrier = pltpu.get_barrier_semaphore()

    def greet(lon_id, lat_id):
        pl.semaphore_signal(barrier, inc=1, device_id=device(lon_id, lat_id), device_id_type=MESH)

    def greet_mates(k, _):
        greet(mate_lon(k), lat)
        return 0

    def greet_groups(k, _):
        greet(remote_lon(k), lat)
        return 0

    lax.fori_loop(1, inner, greet_mates, 0)
    lax.fori_loop(1, outer, greet_groups, 0)

    @pl.when(has_prev)
    def _():
        def greet_side(k, _):
            greet(group * inner + k, prev_lat)
            return 0

        lax.fori_loop(0, inner, greet_side, 0)

    @pl.when(has_next)
    def _():
        def greet_side(k, _):
            greet(group * inner + k, next_lat)
            return 0

        lax.fori_loop(0, inner, greet_side, 0)

    lat_all = merid_ref.shape[1]
    spans = (lat_all, 4 * LANES)
    source = lax.broadcasted_iota(jnp.int32, spans, 0)
    target = lax.broadcasted_iota(jnp.int32, spans, 1)
    second = lat_here - LANES
    own = lat * lat_here + jnp.where(target < LANES, target, target - LANES + second)
    before = (lat - 1) * lat_here + target - 2 * LANES + second
    after = (lat + 1) * lat_here + target - 3 * LANES
    wanted = jnp.where(target < 2 * LANES, own, jnp.where(target < 3 * LANES, before, after))
    repeated = jnp.logical_and(target >= LANES, target < 2 * LANES - second)
    hit = jnp.logical_and(source == wanted, jnp.logical_not(repeated))
    pick = jnp.where(hit, 1.0, 0.0).astype(BF16)
    band_ref[...] = jnp.dot(merid_ref[...], pick, preferred_element_type=F32).astype(BF16)
    levels = vert_ref.shape[0]
    columns_each = LANES // levels
    column = lax.broadcasted_iota(jnp.int32, (LANES, levels), 0)
    level = lax.broadcasted_iota(jnp.int32, (LANES, levels), 1)
    member = jnp.where(column // columns_each == level, 1.0, 0.0).astype(BF16)
    along = (((1,), (1,)), ((), ()))
    by_row = lax.dot_general(member, vert_ref[...], along, preferred_element_type=F32)
    full = lax.dot_general(by_row.astype(BF16), member, along, preferred_element_type=F32)
    row = lax.broadcasted_iota(jnp.int32, (LANES, LANES), 0)
    col = lax.broadcasted_iota(jnp.int32, (LANES, LANES), 1)
    same = row % columns_each == col % columns_each
    level_ref[...] = jnp.where(same, full, 0.0).astype(BF16)

    def clear(slot):
        def clear_lon(i, _):
            inside_halo[slot, i] = jnp.zeros(inside_halo.shape[2:], BF16)
            return 0

        lax.fori_loop(0, inside_halo.shape[1], clear_lon, 0)
        coef_halo[slot] = jnp.zeros(coef_halo.shape[1:], F32)
        lanes = pl.ds((2 + slot) * LANES, LANES)
        entry_ref[:, :, lanes] = jnp.zeros((2, LANES, LANES), F32)

    @pl.when(jnp.logical_not(has_prev))
    def _():
        clear(0)

    @pl.when(jnp.logical_not(has_next))
    def _():
        clear(1)

    sides = has_prev.astype(jnp.int32) + has_next.astype(jnp.int32)
    pl.semaphore_wait(barrier, inner - 1 + outer - 1 + inner * sides)

    def part_copy(k):
        return pltpu.make_async_remote_copy(
            src_ref=ends_ref.at[mate(k)],
            dst_ref=parts.at[place],
            send_sem=send_sem.at[0, k],
            recv_sem=recv_sem.at[0, place],
            device_id=device(mate_lon(k), lat),
            device_id_type=MESH,
        )

    def part_arrival(k):
        return pltpu.make_async_remote_copy(
            src_ref=ends_ref.at[mate(k)],
            dst_ref=parts.at[mate(k)],
            send_sem=send_sem.at[0, k],
            recv_sem=recv_sem.at[0, mate(k)],
            device_id=device(mate_lon(k), lat),
            device_id_type=MESH,
        )

    def send_part(k, _):
        part_copy(k).start()
        return 0

    lax.fori_loop(1, inner, send_part, 0)
    parts[place] = ends_ref[place]

    def side_copies(first, slot, lat_id, base):
        return [
            pltpu.make_async_remote_copy(
                src_ref=inside_hbm.at[:, :, pl.ds(first, LANES)],
                dst_ref=inside_halo.at[slot],
                send_sem=halo_send.at[base],
                recv_sem=halo_recv.at[slot * 2],
                device_id=device(lon, lat_id),
                device_id_type=MESH,
            ),
            pltpu.make_async_remote_copy(
                src_ref=coef_hbm.at[:, :, pl.ds(first, LANES)],
                dst_ref=coef_landing.at[slot],
                send_sem=halo_send.at[base + 1],
                recv_sem=halo_recv.at[slot * 2 + 1],
                device_id=device(lon, lat_id),
                device_id_type=MESH,
            ),
        ]

    @pl.when(has_prev)
    def _():
        for copy in side_copies(0, 1, prev_lat, 0):
            copy.start()

    @pl.when(has_next)
    def _():
        for copy in side_copies(LANES, 0, next_lat, 2):
            copy.start()

    def wait_part(k, _):
        part_arrival(k).wait_recv()
        return 0

    lax.fori_loop(1, inner, wait_part, 0)

    def map_of(ref, index):
        value = ref[index]
        own = 2 * each
        return value[own : own + 1], value[own + 1 : own + 2], value[:each], value[each:own]

    def join(p, near):
        return compose(near, map_of(parts, p))

    loss, cross, east, west = lax.fori_loop(1, inner, join, map_of(parts, 0))
    zero_rows = jnp.zeros((6, 2 * LANES), F32)
    whole = jnp.concatenate([east, west, loss, cross, zero_rows], axis=0)
    joined[...] = whole

    def group_copy(k):
        return pltpu.make_async_remote_copy(
            src_ref=joined,
            dst_ref=groups.at[group],
            send_sem=send_sem.at[1, k],
            recv_sem=recv_sem.at[1, group],
            device_id=device(remote_lon(k), lat),
            device_id_type=MESH,
        )

    def group_arrival(k):
        other = (group + k) % outer
        return pltpu.make_async_remote_copy(
            src_ref=joined,
            dst_ref=groups.at[other],
            send_sem=send_sem.at[1, k],
            recv_sem=recv_sem.at[1, other],
            device_id=device(remote_lon(k), lat),
            device_id_type=MESH,
        )

    def send_group(k, _):
        group_copy(k).start()
        return 0

    lax.fori_loop(1, outer, send_group, 0)
    groups[group] = whole

    def wait_group(k, _):
        group_arrival(k).wait_recv()
        return 0

    lax.fori_loop(1, outer, wait_group, 0)

    zeros = jnp.zeros((each, 2 * LANES), F32)
    none = jnp.zeros((1, 2 * LANES), F32)

    def whole_east(z, carry):
        state, lost = carry
        loss_z, _, east_z, _ = map_of(groups, z)
        return east_z + state - loss_z * state, lost + loss_z - lost * loss_z

    end_state, lost = lax.fori_loop(0, outer, whole_east, (zeros, none))
    first_east = end_state / lost

    def whole_west(z, carry):
        state, kept, east_now = carry
        loss_z, cross_z, east_z, west_z = map_of(groups, z)
        keep_z = 1.0 - loss_z
        state = state + kept * (west_z + cross_z * east_now)
        return state, kept * keep_z, east_z + keep_z * east_now

    west_total, _, _ = lax.fori_loop(0, outer, whole_west, (zeros, none + 1.0, first_east))
    last_west = west_total / lost

    def to_group(z, state):
        loss_z, _, east_z, _ = map_of(groups, z)
        return east_z + state - loss_z * state

    east_here = lax.fori_loop(0, group, to_group, first_east)

    def west_before(z, carry):
        state, kept, east_now = carry
        loss_z, cross_z, east_z, west_z = map_of(groups, z)
        keep_z = 1.0 - loss_z
        state = state + kept * (west_z + cross_z * east_now)
        return state, kept * keep_z, east_z + keep_z * east_now

    _, _, east_after = lax.fori_loop(group, group + 1, west_before, (zeros, none + 1.0, east_here))
    state, kept, _ = lax.fori_loop(group + 1, outer, west_before, (zeros, none + 1.0, east_after))
    west_here = state + kept * last_west

    def inner_east(p, state):
        loss_p, _, east_p, _ = map_of(parts, p)
        solved[p, 0] = state
        return east_p + state - loss_p * state

    lax.fori_loop(0, inner, inner_east, east_here)

    def inner_west(k, state):
        p = inner - 1 - k
        loss_p, cross_p, _, west_p = map_of(parts, p)
        solved[p, 1] = state
        return west_p + cross_p * solved[p, 0] + state - loss_p * state

    lax.fori_loop(0, inner, inner_west, west_here)

    def part_of(index):
        return pl.ds(pl.multiple_of(index * each, each), each)

    def entry_copy(k):
        return pltpu.make_async_remote_copy(
            src_ref=solved.at[mate(k)],
            dst_ref=entry_ref.at[:, part_of(place), pl.ds(0, 2 * LANES)],
            send_sem=send_sem.at[2, k],
            recv_sem=recv_sem.at[2, place],
            device_id=device(mate_lon(k), lat),
            device_id_type=MESH,
        )

    def entry_arrival(k):
        return pltpu.make_async_remote_copy(
            src_ref=solved.at[mate(k)],
            dst_ref=entry_ref.at[:, part_of(mate(k)), pl.ds(0, 2 * LANES)],
            send_sem=send_sem.at[2, k],
            recv_sem=recv_sem.at[2, mate(k)],
            device_id=device(mate_lon(k), lat),
            device_id_type=MESH,
        )

    def side_copy(p, slot, lat_id):
        return pltpu.make_async_remote_copy(
            src_ref=solved.at[p, :, :, pl.ds((1 - slot) * LANES, LANES)],
            dst_ref=entry_ref.at[:, part_of(place), pl.ds((2 + slot) * LANES, LANES)],
            send_sem=send_sem.at[3 + slot, p],
            recv_sem=recv_sem.at[3 + slot, place],
            device_id=device(group * inner + p, lat_id),
            device_id_type=MESH,
        )

    def side_arrival(p, slot):
        return pltpu.make_async_remote_copy(
            src_ref=solved.at[p, :, :, pl.ds((1 - slot) * LANES, LANES)],
            dst_ref=entry_ref.at[:, part_of(p), pl.ds((2 + slot) * LANES, LANES)],
            send_sem=send_sem.at[3 + slot, p],
            recv_sem=recv_sem.at[3 + slot, p],
            device_id=device(group * inner + p, lat),
            device_id_type=MESH,
        )

    @pl.when(has_prev)
    def _():
        def send_side(p, _):
            side_copy(p, 1, prev_lat).start()
            return 0

        lax.fori_loop(0, inner, send_side, 0)

    @pl.when(has_next)
    def _():
        def send_side(p, _):
            side_copy(p, 0, next_lat).start()
            return 0

        lax.fori_loop(0, inner, send_side, 0)

    def send_entry(k, _):
        entry_copy(k).start()
        return 0

    lax.fori_loop(1, inner, send_entry, 0)
    entry_ref[:, part_of(place), pl.ds(0, 2 * LANES)] = solved[place]

    def wait_entry(k, _):
        entry_arrival(k).wait_recv()
        return 0

    lax.fori_loop(1, inner, wait_entry, 0)

    @pl.when(has_prev)
    def _():
        def wait_side(p, _):
            side_arrival(p, 0).wait_recv()
            return 0

        lax.fori_loop(0, inner, wait_side, 0)

    @pl.when(has_next)
    def _():
        def wait_side(p, _):
            side_arrival(p, 1).wait_recv()
            return 0

        lax.fori_loop(0, inner, wait_side, 0)

    @pl.when(has_prev)
    def _():
        inside_copy, coef_copy = side_copies(0, 0, prev_lat, 0)
        coef_copy.wait_recv()
        coef_halo[0] = coef_landing[0].astype(F32)
        inside_copy.wait_recv()
        for copy in side_copies(0, 1, prev_lat, 0):
            copy.wait_send()

    @pl.when(has_next)
    def _():
        inside_copy, coef_copy = side_copies(LANES, 1, next_lat, 2)
        coef_copy.wait_recv()
        coef_halo[1] = coef_landing[1].astype(F32)
        inside_copy.wait_recv()
        for copy in side_copies(LANES, 0, next_lat, 2):
            copy.wait_send()

    def drain_inner(k, _):
        part_copy(k).wait_send()
        entry_copy(k).wait_send()
        return 0

    def drain_outer(k, _):
        group_copy(k).wait_send()
        return 0

    lax.fori_loop(1, inner, drain_inner, 0)
    lax.fori_loop(1, outer, drain_outer, 0)

    @pl.when(has_prev)
    def _():
        def drain(p, _):
            side_copy(p, 1, prev_lat).wait_send()
            return 0

        lax.fori_loop(0, inner, drain, 0)

    @pl.when(has_next)
    def _():
        def drain(p, _):
            side_copy(p, 0, next_lat).wait_send()
            return 0

        lax.fori_loop(0, inner, drain, 0)


def run_exchange(mesh, ends, inside, coef_small, merid, vert):
    lons, lats = mesh.shape["lon"], mesh.shape["lat"]
    inner, height, width = ends.shape
    outer = lons // inner
    lat_here = merid.shape[0]
    lon_here = inside.shape[0]
    vmem = pl.BlockSpec(memory_space=pltpu.VMEM)
    hbm = pl.BlockSpec(memory_space=pl.ANY)
    most = max(inner, outer)
    return pl.pallas_call(
        functools.partial(exchange_kernel, inner, outer, lats),
        name="loop_exchange",
        out_shape=(
            jax.ShapeDtypeStruct((2, LANES, 4 * LANES), F32),
            jax.ShapeDtypeStruct((2, lon_here, LANES, LANES), BF16),
            jax.ShapeDtypeStruct((2, 2, coef_small.shape[1], LANES), F32),
            jax.ShapeDtypeStruct((lat_here, 4 * LANES), BF16),
            jax.ShapeDtypeStruct((LANES, LANES), BF16),
        ),
        in_specs=[vmem, hbm, hbm, vmem, vmem],
        out_specs=(vmem, vmem, vmem, vmem, vmem),
        scratch_shapes=[
            pltpu.VMEM((2, 2, coef_small.shape[1], LANES), BF16),
            pltpu.VMEM((inner, height, width), F32),
            pltpu.VMEM((height, width), F32),
            pltpu.VMEM((outer, height, width), F32),
            pltpu.VMEM((inner, 2, LANES // inner, width), F32),
            pltpu.SemaphoreType.DMA((5, most)),
            pltpu.SemaphoreType.DMA((5, most)),
            pltpu.SemaphoreType.DMA((4,)),
            pltpu.SemaphoreType.DMA((4,)),
        ],
        compiler_params=pltpu.CompilerParams(
            collective_id=0, has_side_effects=True, vmem_limit_bytes=24 << 20
        ),
    )(ends, inside, coef_small, merid, vert)


def combine_kernel(
    batch,
    levels,
    inside_ref,
    before_ref,
    after_ref,
    coef_ref,
    coef_before_ref,
    coef_after_ref,
    entry_ref,
    band_ref,
    level_ref,
    out_ref,
    zonal,
):
    each = LANES // levels
    group = 4
    along = (((1,), (1,)), ((), ()))

    def fill(first):
        for level in range(levels):
            rows = pl.ds(level * each, each)
            for tile in range(4):
                lanes = pl.ds(tile * LANES, LANES)
                east, west = entry_ref[0, rows, lanes], entry_ref[1, rows, lanes]
                for j in range(first, first + group):
                    row = j * levels + level
                    if tile < 2:
                        inside = inside_ref[j, rows, lanes]
                        cross = coef_ref[0, j, pl.ds(level, 1), lanes]
                        kept = coef_ref[1, j, pl.ds(level, 1), lanes]
                    else:
                        halo, coef = (
                            (before_ref, coef_before_ref),
                            (after_ref, coef_after_ref),
                        )[tile - 2]
                        inside = halo[0, j, rows, :].astype(F32)
                        cross = coef[0, 0, pl.ds(row, 1), :]
                        kept = coef[0, 1, pl.ds(row, 1), :]
                    field = inside + cross * east + kept * west
                    zonal[j // 2, pl.ds(j % 2 * LANES + level * each, each), lanes] = (
                        field.astype(BF16)
                    )

    def multiply(first):
        for pair in range(first // 2, (first + group) // 2):
            merid = lax.dot_general(
                band_ref[...], zonal[pair], along, preferred_element_type=F32
            ).astype(BF16)
            for side in range(2):
                out_ref[2 * pair + side] = jnp.dot(
                    merid[:, side * LANES : (side + 1) * LANES],
                    level_ref[...],
                    preferred_element_type=F32,
                ).astype(BF16)

    fill(0)
    for first in range(group, batch, group):
        fill(first)
        multiply(first - group)
    multiply(batch - group)


def run_combine(inside, inside_halo, coef, coef_halo, entry, band_tile, level_map):
    lon_here, _, width = inside.shape
    levels = coef.shape[2]
    lat_here = band_tile.shape[0]
    batch = 8
    return pl.pallas_call(
        functools.partial(combine_kernel, batch, levels),
        name="band_product",
        grid=(lon_here // batch,),
        out_shape=jax.ShapeDtypeStruct((lon_here, lat_here, LANES), BF16),
        in_specs=[
            pl.BlockSpec((batch, LANES, width), lambda t: (t, 0, 0)),
            pl.BlockSpec((1, batch, LANES, LANES), lambda t: (0, t, 0, 0)),
            pl.BlockSpec((1, batch, LANES, LANES), lambda t: (1, t, 0, 0)),
            pl.BlockSpec((2, batch, levels, width), lambda t: (0, t, 0, 0)),
            pl.BlockSpec((1, 2, batch * levels, LANES), lambda t: (0, 0, t, 0)),
            pl.BlockSpec((1, 2, batch * levels, LANES), lambda t: (1, 0, t, 0)),
            pl.BlockSpec(entry.shape, lambda t: (0, 0, 0)),
            pl.BlockSpec(band_tile.shape, lambda t: (0, 0)),
            pl.BlockSpec(level_map.shape, lambda t: (0, 0)),
        ],
        out_specs=pl.BlockSpec((batch, lat_here, LANES), lambda t: (t, 0, 0)),
        scratch_shapes=[pltpu.VMEM((batch // 2, 2 * LANES, 4 * LANES), BF16)],
        compiler_params=pltpu.CompilerParams(vmem_limit_bytes=20 << 20),
    )(inside, inside_halo, inside_halo, coef, coef_halo, coef_halo, entry, band_tile, level_map)


def solution(mesh):
    def per_device(sketch_bits, rates, merid_matrix, vert_matrix):
        ends, inside, inside_small, coef, coef_small = run_filters(rates, sketch_bits)
        entry, inside_halo, coef_halo, band_tile, level_map = run_exchange(
            mesh, ends, inside_small, coef_small, merid_matrix, vert_matrix
        )
        return run_combine(inside, inside_halo, coef, coef_halo, entry, band_tile, level_map)

    in_specs = (P("lon", "lat", None), P("lon", None, "lat"), P("lat", None), P())
    out_specs = P("lon", "lat", None)
    return jax.shard_map(
        per_device, mesh=mesh, in_specs=in_specs, out_specs=out_specs, check_vma=False
    )
```

time: 55.9 us -> 56.4 us (level)
    pallas_call x2, Pallas kernels: 44.5 us -> 48 us  [the longest x1 40.9 us: run_exchange(): pl.pallas_call(functools.partial(exchange_kernel, inner, outer, lats), na...]
    pallas_call x1, Pallas kernels: 11.3 us -> 8.3 us  [run_combine(): pl.pallas_call(functools.partial(combine_kernel, batch, levels), name='ba...]
where the time goes in v3:
time: 56.4 us; the launch traced here: 56.3 us
  Pallas kernels  56.3 us (100%)
    pallas_call x1, Pallas kernels, run_exchange(): pl.pallas_call(functools.partial(exchange_kernel, inner, outer, lats), na...  40.9 us
    pallas_call x1, Pallas kernels, run_combine(): pl.pallas_call(functools.partial(combine_kernel, batch, levels), name='ba...  8.3 us
    pallas_call x1, Pallas kernels, run_filters(): pl.pallas_call(filter_kernel, name='zonal_filters', out_shape=(jax.ShapeD...  7.15 us

profile of v3, /device:TPU:1, one launch (start us, length us, event | category | flops | bytes accessed | tf_op | source)
XLA Modules:
  0.0 56.3 jit_solution(16556615347860155670)
XLA Ops:
  0.0 0.0 copy-start.1
  0.0 0.0 copy-start
  0.0 7.2 %zonal_filters.1 = (f32[8,40,256]{2,1,0:T(8,128)S(1)}, f32[48,128,256]{2,1,0:T(8,128)S(1)}, bf16[48,128,256]{2,1,0:T(8,128)(2,1)S(1)}, f32[2,48,8,256]{3,2,1,0:T(8,128)S(1)}, bf16[2,384,256]{2,1,0:T(8,128)(2,1)S(1)}) custom-call(f32[48,8,192]{2,1,0:T(8,128)} %rates_hbm.1, s32[48,192,128]{2,1,0:T(8,128)} %bits_hbm.1), custom_call_target="tpu_custom_call" | custom-call | tf_op jit(solution)/shard_map/zonal_filters/pallas_call | solution.py:142
  7.2 0.0 copy-done.1
  7.2 0.0 copy-done
  7.2 40.9 %loop_exchange.1 = (f32[2,128,512]{2,1,0:T(8,128)S(1)}, bf16[2,48,128,128]{3,2,1,0:T(8,128)(2,1)S(1)}, f32[2,2,384,128]{3,2,1,0:T(8,128)S(1)}, bf16[192,512]{1,0:T(8,128)(2,1)S(1)}, bf16[128,128]{1,0:T(8,128)(2,1)S(1)}) custom-call(f32[8,40,256]{2,1,0:T(8,128)S(1)} %get-tuple-element.16.ends_ref, bf16[48,128,256]{2,1,0:T(8,128)(2,1)S(1)} %get-tuple-element.17.inside_hbm, ...), custom_call_target="tpu_custom_call" | custom-call | tf_op jit(solution)/shard_map/loop_exchange/pallas_call | solution.py:612
  48.0 8.3 %band_product.1 = bf16[48,192,128]{2,1,0:T(8,128)(2,1)} custom-call(f32[48,128,256]{2,1,0:T(8,128)S(1)} %get-tuple-element.15.inside_ref, bf16[2,48,128,128]{3,2,1,0:T(8,128)(2,1)S(1)} %get-tuple-element.19.before_ref.after_ref, bf16[2,48,128,128]{3,2,1,0:T(8,128)(2,1)S(1)} %get-tuple-element.19.before_ref.after_ref, ...), custom_call_target="tpu_custom_call" | custom-call | tf_op jit(solution)/shard_map/band_product/pallas_call | solution.py:709
Async XLA Ops:
  0.0 7.2 %copy-start.1 = (bf16[8,8]{1,0:T(8,128)(2,1)S(1)}, bf16[8,8]{1,0:T(8,128)(2,1)}, u32[]{:S(2)}) copy-start(bf16[8,8]{1,0:T(8,128)(2,1)} %vert_ref.1) | copy-start | bytes 388
  0.0 7.2 %copy-start = (bf16[192,768]{1,0:T(8,128)(2,1)S(1)}, bf16[192,768]{1,0:T(8,128)(2,1)}, u32[]{:S(2)}) copy-start(bf16[192,768]{1,0:T(8,128)(2,1)} %merid_ref.1) | copy-start | bytes 884740
